TPU v7x, 256 devices: a whole 4x4x8 slice. The times are simulated.
256 devices in a mesh: tm: 32 (over x_hi, z, core), stripe: 8 (over x_lo, y).
Axes of the slice: x: 4 (x_hi: 2, x_lo: 2; x = x_hi * 2 + x_lo), y: 4, z: 8, core: 2. Of those that a mesh axis runs over, the one named last changes fastest.
Arguments:
- data_vec: float32 [128, 2, 512], P('tm', None, 'stripe'), may hold values from -6 to 6
- kernel: bfloat16 [128, 2, 512, 8192], P('tm', None, None, 'stripe'), may hold values from -0.1875 to 0.1875
- time_spectrum: float32 [128], P('tm'), may hold values from 0.25 to 2
- prior_spectrum: float32 [128, 64], replicated, may hold values from 0.05 to 1
- noise_var: float32 [512], P('stripe'), may hold values from 0.1 to 1
Outputs:
- hessian_vec: float32 [128, 2, 512], P('tm', None, 'stripe')
All inputs are finite; a program needn't handle non-finite values.
Results may differ from a plain program's by a relative error of at most 0.0022.
Values may be sent and summed in bfloat16 or wider, within the bound.
No kernel may reach another device: no remote copies, remote signals or barrier semaphores. Data moves between devices by JAX's collectives and lax.ppermute only.
A program may use at most 64 MiB of HBM per device.

v0:
```python
import math

import jax
import jax.numpy as jnp
from jax import lax
from jax.sharding import PartitionSpec as P

precise = lax.Precision.HIGHEST


def angle_tables(freq_ids, time_ids, length):
    product = freq_ids[:, None] * time_ids[None, :] % (2 * length)
    angles = product.astype(jnp.float32) * (math.pi / length)
    return (jnp.cos(angles), jnp.sin(angles))


def sine_matrix(length):
    numbers = jnp.arange(length, dtype=jnp.int32) + 1
    product = numbers[:, None] * numbers[None, :] % (2 * (length + 1))
    return jnp.sin(product.astype(jnp.float32) * (math.pi / (length + 1))) * math.sqrt(
        2.0 / (length + 1)
    )


def spectra_term(values, tm_index, time_total, count):
    steps_here = values.shape[0]
    freq_ids = jnp.arange(count, dtype=jnp.int32)
    time_ids = tm_index * steps_here + jnp.arange(steps_here, dtype=jnp.int32)
    cosine, sine_part = angle_tables(freq_ids, time_ids, time_total)
    real_part = jnp.einsum("kt,tns->kns", cosine, values, precision=precise)
    imag_part = -jnp.einsum("kt,tns->kns", sine_part, values, precision=precise)
    return jnp.stack([real_part, imag_part], 1) / math.sqrt(time_total)


def times_term(images, tm_index, time_total, count):
    freqs_here = images.shape[0]
    time_ids = jnp.arange(count, dtype=jnp.int32)
    freq_ids = tm_index * freqs_here + jnp.arange(freqs_here, dtype=jnp.int32)
    cosine, sine_part = angle_tables(freq_ids, time_ids, time_total)
    time_real = jnp.einsum("kt,kns->tns", cosine, images[:, 0], precision=precise)
    time_imag = jnp.einsum("kt,kns->tns", sine_part, images[:, 1], precision=precise)
    return (time_real - time_imag) / math.sqrt(time_total)


def grid_prior(grid_stack, row_sine, column_sine, spectrum):
    forward_grid = jnp.einsum("ai,mij->maj", row_sine, grid_stack, precision=precise)
    forward_grid = (
        jnp.einsum("maj,jb->mab", forward_grid, column_sine, precision=precise) * spectrum
    )
    backward_grid = jnp.einsum("ia,mab->mib", row_sine, forward_grid, precision=precise)
    return jnp.einsum("mib,bj->mij", backward_grid, column_sine, precision=precise)


def shards(data_vec, kernel, time_spectrum, prior_spectrum, noise_var):
    tm_index = lax.axis_index("tm")
    stripes = lax.axis_size("stripe")
    steps_here = data_vec.shape[0]
    vectors = data_vec.shape[1]
    freqs_here = kernel.shape[0]
    points_here = kernel.shape[3]
    time_total = steps_here * lax.axis_size("tm")
    rows_all = prior_spectrum.shape[0]
    columns = prior_spectrum.shape[1]
    rows_here = points_here // columns
    data_all = lax.all_gather(data_vec, "stripe", axis=2, tiled=True)
    summed = lax.psum_scatter(
        spectra_term(data_all, tm_index, time_total, freqs_here * lax.axis_size("tm")),
        "tm",
        scatter_dimension=0,
        tiled=True,
    )
    spectra = summed.astype(jnp.bfloat16)
    swapped = jnp.stack([spectra[:, 1], -spectra[:, 0]], 1)
    adj_real = jnp.einsum("kcsp,kcns->knp", kernel, spectra, preferred_element_type=jnp.float32)
    adj_imag = jnp.einsum("kcsp,kcns->knp", kernel, swapped, preferred_element_type=jnp.float32)
    adjoint = jnp.stack([adj_real, adj_imag], 1) * time_spectrum[:, None, None, None]
    row_sine = sine_matrix(rows_all)
    column_sine = sine_matrix(columns)
    item_count = freqs_here * 2 * vectors
    per_group = item_count // stripes
    grid_stack = adjoint.reshape(stripes, per_group, rows_here, columns)
    shaped = grid_prior(
        lax.all_to_all(grid_stack, "stripe", split_axis=0, concat_axis=2, tiled=True)[0],
        row_sine,
        column_sine,
        prior_spectrum,
    )
    smoothed = lax.all_to_all(
        shaped[None].astype(jnp.bfloat16), "stripe", split_axis=2, concat_axis=0, tiled=True
    ).astype(jnp.float32)
    smoothed_bf = smoothed.reshape(freqs_here, 2, vectors, points_here).astype(jnp.bfloat16)
    pair_real = jnp.stack([smoothed_bf[:, 0], -smoothed_bf[:, 1]], 1)
    pair_imag = jnp.stack([smoothed_bf[:, 1], smoothed_bf[:, 0]], 1)
    out_real = jnp.einsum("kcsp,kcnp->kns", kernel, pair_real, preferred_element_type=jnp.float32)
    out_imag = jnp.einsum("kcsp,kcnp->kns", kernel, pair_imag, preferred_element_type=jnp.float32)
    images = jnp.stack([out_real, out_imag], 1)
    time_sums = lax.psum_scatter(
        times_term(images, tm_index, time_total, steps_here * lax.axis_size("tm")),
        "tm",
        scatter_dimension=0,
        tiled=True,
    )
    result = lax.psum_scatter(time_sums, "stripe", scatter_dimension=2, tiled=True)
    return result + noise_var[None, None, :] * data_vec


def solution(mesh):
    return jax.shard_map(
        shards,
        mesh=mesh,
        in_specs=(
            P("tm", None, "stripe"),
            P("tm", None, None, "stripe"),
            P("tm"),
            P(),
            P("stripe"),
        ),
        out_specs=P("tm", None, "stripe"),
        check_vma=False,
    )
```

profile of v0, /device:TPU:1, one launch (start us, length us, event | category | flops | bytes accessed | tf_op | source)
XLA Modules:
  0.0 534.4 jit_solution(7578918533974694577)
XLA Ops:
  6.5 0.8 copy.22
  7.3 24.6 %all_gather.3 = f32[4,2,512]{0,1,2:T(2,128)S(1)} all-gather(f32[4,2,64]{0,1,2:T(2,128)S(1)} %copy.22), channel_id=1, replica_groups=mesh['tm'=32,'stripe'=8] {'stripe'}, dimensions={2}, use_global_device_ids=true | all-gather | bytes 18432 | tf_op jit(solution)/shard_map/all_gather | solution.py:65
  31.9 0.2 copy.23
  32.1 0.8 convolution_bitcast_fusion
  32.9 0.7 fusion.1
  33.8 141.8 %all-reduce.6 = bf16[128,2,2,512]{3,0,2,1:T(8,128)(2,1)S(1)} all-reduce(f32[128,2,2,512]{3,0,2,1:T(8,128)S(1)} %maximum_multiply_fusion), channel_id=2, replica_groups=mesh['tm'=32,'stripe'=8] {'tm'}, use_global_device_ids=true, to_apply=%region_0.1.clone | all-reduce | flops 262144 | bytes 1572864
  175.6 1.3 dynamic-slice
  177.7 4.7 convolution_bitcast_fusion.4
  182.4 0.9 copy-done
  183.3 1.2 convolution_bitcast_fusion.3
  184.6 0.1 stack.38
  185.0 0.7 reshape.53
  185.7 3.8 all-to-all-start
  189.6 5.1 all-to-all-done
  194.7 0.5 broadcast.63
  195.2 0.8 reduce
  196.1 0.6 convolution_bitcast_fusion.2
  196.7 0.4 convolution_multiply_fusion
  197.1 0.6 convolution_bitcast_fusion.1
  197.6 0.4 fusion.2
  198.3 7.5 %all_to_all.33 = bf16[8,2,1024]{2,1,0:T(2,128)(2,1)S(1)} all-to-all(bf16[8,2,1024]{2,1,0:T(2,128)(2,1)S(1)} %reshape.55), channel_id=1, replica_groups=mesh['tm'=32,'stripe'=8] {'stripe'}, dimensions={0} | all-to-all | bytes 65536 | tf_op jit(solution)/shard_map/all_to_all | solution.py:88
  206.2 5.7 %convolution_bitcast_fusion.6 = f32[4,2,512]{2,1,0:T(2,128)S(1)} fusion(bf16[4,2,512,1024]{3,2,1,0:T(8,128)(2,1)} %param.6, bf16[4,1,2,1024]{3,2,1,0:T(2,128)(2,1)S(1)} %get-tuple-element.5, bf16[4,1,2,1024]{3,2,1,0:T(2,128)(2,1)S(1)} %copy.48), kind=kOutput, calls=%fused_computation.13 | convolution fusion | flops 16842752 | bytes 8437760 | tf_op jit(solution)/shard_map/kcsp,kcnp->kns/dot_general | solution.py:94
  211.8 0.8 fusion.45
  212.6 5.7 %convolution_bitcast_fusion.5 = f32[4,2,512]{2,1,0:T(2,128)S(1)} fusion(bf16[4,2,512,1024]{3,2,1,0:T(8,128)(2,1)} %param.6, bf16[4,1,2,1024]{3,2,1,0:T(2,128)(2,1)S(1)} %copy.48, bf16[4,1,2,1024]{3,2,1,0:T(2,128)(2,1)S(1)} %get-tuple-element.6), kind=kOutput, calls=%fused_computation.12 | convolution fusion | flops 16842752 | bytes 8437760 | tf_op jit(solution)/shard_map/kcsp,kcnp->kns/dot_general | solution.py:95
  218.3 1.6 fusion
  219.9 270.4 %all-reduce.5.cloned.1.call-done = f32[128,2,512]{2,0,1:T(8,128)} async-done(((f32[128,2,512]{2,0,1:T(8,128)}), f32[128,2,512]{2,0,1:T(8,128)}) %all-reduce.5.cloned.1.call-update) | async-done | bytes 524304
  490.3 0.8 constant_dynamic-slice_fusion
  491.0 0.3 copy.46
  491.3 1.0 reshape.49
  492.3 33.6 %reduce-scatter.6.cloned.1.call-done = f32[64,8]{1,0:T(8,128)} async-done(((f32[512,8]{1,0:T(8,128)}), f32[64,8]{1,0:T(8,128)}) %reduce-scatter.6.cloned.1.call-update) | async-done | bytes 2064
  526.0 0.9 reshape.50
  526.9 0.6 copy.35
  (37 shorter events, 1.4 us)
Async XLA Ops:
  177.5 5.8 %copy-start = (bf16[4,2,512,1024]{3,2,1,0:T(8,128)(2,1)S(1)}, bf16[4,2,512,1024]{3,2,1,0:T(8,128)(2,1)}, u32[]{:S(2)}) copy-start(bf16[4,2,512,1024]{3,2,1,0:T(8,128)(2,1)} %param.6) | copy-start | bytes 25165828
  177.6 7.1 %copy-start.3 = (f32[4]{0:T(128)S(1)}, f32[4]{0:T(128)}, u32[]{:S(2)}) copy-start(f32[4]{0:T(128)} %param.7) | copy-start | bytes 52
  177.6 19.0 %copy-start.1 = (f32[128,64]{0,1:T(8,128)S(1)}, f32[128,64]{0,1:T(8,128)}, u32[]{:S(2)}) copy-start(f32[128,64]{0,1:T(8,128)} %param.8) | copy-start | bytes 98308
  185.7 9.0 %all-to-all-start = ((f32[8,1,2048]{2,1,0:T(1,128)}), f32[8,1,2048]{2,1,0:T(1,128)S(1)}, u32[]{:S(2)}, u32[]{:S(2)}) async-start(f32[8,1,2048]{2,1,0:T(1,128)} %reshape.53), calls=%async_computation | async-start | bytes 131072 | tf_op jit(solution)/shard_map/all_to_all | solution.py:83
  189.5 300.8 %all-reduce.5.cloned.1.call-start = ((), (), s32[]{:S(2)}) async-start(), calls=%async_computation.4 | async-start | bytes 1048576
  206.2 320.8 %copy-start.2 = (f32[4,2,64]{2,1,0:T(2,128)S(1)}, f32[4,2,64]{2,1,0:T(2,128)}, u32[]{:S(2)}) copy-start(f32[4,2,64]{2,1,0:T(2,128)} %param.5) | copy-start | bytes 6148
  206.2 320.8 %copy-start.4 = (f32[64]{0:T(128)S(1)}, f32[64]{0:T(128)}, u32[]{:S(2)}) copy-start(f32[64]{0:T(128)} %param.9) | copy-start | bytes 772
  219.8 306.1 %reduce-scatter.6.cloned.1.call-start = ((), (), s32[]{:S(2)}) async-start(), calls=%async_computation.3 | async-start | bytes 294912
Sparse Core Ops, SparseCore 0:
  220.0 270.2 all-reduce.4
  492.8 33.1 reduce-scatter.5
where the time goes:
time: 539 us; the launch traced here: 534 us
  waiting for transfers between devices  309 us (57%)
  blocking collectives  174 us (32%)
  matrix products  23 us (4%)
  between operations  14.3 us (3%)
  local copies, waits for them, and re-layouts  9.02 us (2%)
    unnamed x4, waiting for transfers between devices  304 us
    unnamed x1, blocking collectives  142 us
    all_gather x1, blocking collectives, shards(): data_all = lax.all_gather(data_vec, 'stripe', axis=2, tiled=True)  24.6 us
  transfers between devices with their start and end apart: 3, of which 3 were waited for; matrix products, arithmetic and copies ran while one was open for 0% of the time, Pallas kernels for 0%

commit v1 on v0

v1 whole, which is shorter than its diff:
```python
import functools
import math

import jax
import jax.numpy as jnp
import numpy as np
from jax import lax
from jax.experimental import pallas as pl
from jax.experimental.pallas import tpu as pltpu
from jax.sharding import PartitionSpec as P

exact = lax.Precision.HIGHEST
f32 = jnp.float32
bf16 = jnp.bfloat16


def whole():
    return pl.BlockSpec(memory_space=pltpu.VMEM)


def scalars():
    return pl.BlockSpec(memory_space=pltpu.SMEM)


def call(body, out_shape, operands, specs, scratch=()):
    return pl.pallas_call(
        body,
        out_shape=out_shape,
        in_specs=list(specs),
        out_specs=whole(),
        scratch_shapes=list(scratch),
    )(*operands)


def mm(a, b, dims=((1,), (0,)), precision=exact):
    return lax.dot_general(
        a, b, (dims, ((), ())), precision=precision, preferred_element_type=f32
    )


def fourier_table(blocks):
    steps = np.arange(128)
    angles = np.outer(steps, steps) % 256 * (math.pi / 128)
    pair = np.stack([np.cos(angles), -np.sin(angles)]) / math.sqrt(128)
    pair = pair.reshape(2, blocks, 128 // blocks, 128).transpose(1, 0, 2, 3)
    return pair.reshape(blocks, 2 * (128 // blocks), 128).astype(np.float32)


def sine_matrix(length):
    numbers = np.arange(length) + 1
    product = np.outer(numbers, numbers) % (2 * (length + 1))
    return np.sin(product * (math.pi / (length + 1))) * math.sqrt(2.0 / (length + 1))


def row_order():
    stripe, parity, c = np.meshgrid(np.arange(8), np.arange(2), np.arange(8), indexing="ij")
    return (stripe * 16 + 2 * c + parity).reshape(-1)


def low_half(shape):
    return lax.broadcasted_iota(jnp.int32, shape, len(shape) - 1) < 64


def swap_halves(first, second):
    keep = low_half(first.shape)
    low = jnp.where(keep, first, pltpu.roll(second, 64, 1))
    high = jnp.where(keep, pltpu.roll(first, 64, 1), second)
    return low, high


def spread_body(data_ref, out_ref):
    flat = jnp.concatenate([data_ref[:, 0, :], data_ref[:, 1, :]], axis=1)
    two = jnp.concatenate([flat, flat], axis=0)
    for r in range(16):
        out_ref[r * 8 : r * 8 + 8, :] = two


def spectra_body(data_ref, table_ref, out_ref):
    tm = lax.axis_index("tm")
    spectra = mm(table_ref[tm], data_ref[...]).astype(bf16)
    for r in range(8):
        out_ref[r] = spectra


def adjoint_body(gathered_ref, kernel_ref, scale_ref, column_ref, out_ref, grid_ref):
    parts = [[], []]
    for j in range(4):
        first = gathered_ref[2 * j].astype(f32)
        second = gathered_ref[2 * j + 1].astype(f32)
        low, high = swap_halves(first, second)
        parts[0].append(low)
        parts[1].append(high)
    rows = [jnp.concatenate(part, axis=1) for part in parts]
    sub = lax.broadcasted_iota(jnp.int32, (8, 512), 0)
    turned = [jnp.where(sub < 4, pltpu.roll(r, 4, 0), -pltpu.roll(r, 4, 0)) for r in rows]
    straight = jnp.concatenate(rows, axis=0)
    turned = jnp.concatenate(turned, axis=0)
    freq = lax.broadcasted_iota(jnp.int32, (16, 512), 0) % 4
    total = None
    for k in range(4):
        for c, source in enumerate((straight, turned)):
            left = jnp.where(freq == k, source, 0.0).astype(bf16)
            term = mm(left, kernel_ref[k, c], precision=None)
            total = term if total is None else total + term
    row = lax.broadcasted_iota(jnp.int32, (16, 1024), 0) % 4
    scale = jnp.where(
        row < 2,
        jnp.where(row == 0, scale_ref[0], scale_ref[1]),
        jnp.where(row == 2, scale_ref[2], scale_ref[3]),
    )
    total = total * scale
    stack = jnp.concatenate([total[:, c * 128 : c * 128 + 128] for c in range(8)], axis=0)
    grid_ref[...] = mm(stack, column_ref[...])
    for m in range(8):
        first = grid_ref[pl.ds(2 * m, 8, stride=16), :]
        second = grid_ref[pl.ds(2 * m + 1, 8, stride=16), :]
        low, high = swap_halves(first, second)
        for r in range(8):
            out_ref[r, 0:8, m * 128 : m * 128 + 128] = low
            out_ref[r, 8:16, m * 128 : m * 128 + 128] = high


def images_body(
    grids_ref, kernel_ref, prior_ref, forward_ref, backward_ref, column_ref, out_ref, grid_ref
):
    stripe = lax.axis_index("stripe")
    modes = mm(forward_ref[...], grids_ref[...])
    prior = prior_ref[...].T
    prior = jnp.concatenate([prior, prior], axis=1)
    modes = modes * jnp.concatenate([prior] * 8, axis=1)
    back = mm(backward_ref[pl.ds(stripe * 16, 16), :], modes)
    for m in range(8):
        first, second = swap_halves(
            back[0:8, m * 128 : m * 128 + 128], back[8:16, m * 128 : m * 128 + 128]
        )
        grid_ref[pl.ds(2 * m, 8, stride=16), :] = first
        grid_ref[pl.ds(2 * m + 1, 8, stride=16), :] = second
    smooth = mm(grid_ref[...], column_ref[...])
    smooth = jnp.concatenate([smooth[c * 16 : c * 16 + 16, :] for c in range(8)], axis=1)
    sub = lax.broadcasted_iota(jnp.int32, (8, 1024), 0)
    turned = []
    for n in range(2):
        moved = pltpu.roll(smooth[n * 8 : n * 8 + 8, :], 4, 0)
        turned.append(jnp.where(sub < 4, -moved, moved))
    turned = jnp.concatenate(turned, axis=0)
    freq = lax.broadcasted_iota(jnp.int32, (16, 1024), 0) % 4
    total = None
    for k in range(4):
        for c, source in enumerate((smooth, turned)):
            left = jnp.where(freq == k, source, 0.0).astype(bf16)
            term = mm(left, kernel_ref[k, c], ((1,), (1,)), precision=None)
            total = term if total is None else total + term
    for j in range(4):
        low, high = swap_halves(
            total[0:8, j * 128 : j * 128 + 128], total[8:16, j * 128 : j * 128 + 128]
        )
        out_ref[2 * j] = low
        out_ref[2 * j + 1] = high


def times_body(images_ref, table_ref, out_ref):
    tm = lax.axis_index("tm")
    total = images_ref[0]
    for r in range(1, 8):
        total = total + images_ref[r]
    out_ref[...] = mm(table_ref[tm], total, ((0,), (0,)))


def finish_body(sums_ref, data_ref, noise_ref, out_ref):
    total = sums_ref[0:8, :]
    for r in range(1, 16):
        total = total + sums_ref[r * 8 : r * 8 + 8, :]
    total = total[0:4, :] + total[4:8, :]
    noise = noise_ref[...]
    out_ref[:, 0, :] = total[:, 0:64] + noise * data_ref[:, 0, :]
    out_ref[:, 1, :] = total[:, 64:128] + noise * data_ref[:, 1, :]


def exchange(x, axis):
    return lax.all_to_all(x, axis, 0, 0, tiled=True)


def shards(data_vec, kernel, time_spectrum, prior_spectrum, noise_var):
    table = jnp.asarray(fourier_table(32))
    rows = sine_matrix(128)
    order = row_order()
    backward = jnp.asarray(rows[order].astype(np.float32))
    forward = jnp.asarray(rows[:, order].astype(np.float32))
    columns = sine_matrix(64)
    column = jnp.asarray(np.kron(np.eye(2), columns).astype(np.float32))

    spread = call(spread_body, jax.ShapeDtypeStruct((128, 128), f32), (data_vec,), (whole(),))
    by_time = exchange(spread.reshape(32, 4, 128), "tm").reshape(128, 128)
    spectra = call(
        spectra_body,
        jax.ShapeDtypeStruct((8, 8, 128), bf16),
        (by_time, table),
        (whole(), whole()),
    )
    gathered = exchange(spectra, "stripe")
    grids = call(
        adjoint_body,
        jax.ShapeDtypeStruct((8, 16, 1024), f32),
        (gathered, kernel, time_spectrum, column),
        (whole(), whole(), scalars(), whole()),
        (pltpu.VMEM((128, 128), f32),),
    )
    grids = exchange(grids, "stripe").reshape(128, 1024)
    images = call(
        images_body,
        jax.ShapeDtypeStruct((8, 8, 128), f32),
        (grids, kernel, prior_spectrum.T, forward, backward, column),
        (whole(),) * 6,
        (pltpu.VMEM((128, 128), f32),),
    )
    images = exchange(images, "stripe")
    sums = call(
        times_body, jax.ShapeDtypeStruct((128, 128), f32), (images, table), (whole(), whole())
    )
    sums = exchange(sums.reshape(32, 4, 128), "tm").reshape(128, 128)
    return call(
        finish_body,
        jax.ShapeDtypeStruct((4, 2, 64), f32),
        (sums, data_vec, noise_var.reshape(1, 64)),
        (whole(),) * 3,
    )


def solution(mesh):
    return jax.shard_map(
        shards,
        mesh=mesh,
        in_specs=(
            P("tm", None, "stripe"),
            P("tm", None, None, "stripe"),
            P("tm"),
            P(),
            P("stripe"),
        ),
        out_specs=P("tm", None, "stripe"),
        check_vma=False,
    )
```

time: 539 us -> 91.3 us (0.17)
  waiting for transfers between devices: 309 us -> 0 us
  blocking collectives: 174 us -> 71.1 us
  matrix products: 23 us -> 0 us
  Pallas kernels: 0 us -> 19.7 us
  between operations: 14.3 us -> 0.01 us
  local copies, waits for them, and re-layouts: 9.02 us -> 0 us
    unnamed x4 -> x0, waiting for transfers between devices: 304 us -> none
    unnamed x1 -> x0, blocking collectives: 142 us -> none
    all_to_all x1 -> x5, blocking collectives: 7.48 us -> 71.1 us  [exchange(): return lax.all_to_all(x, axis, 0, 0, tiled=True)]
    all_gather x1 -> x0, blocking collectives: 24.6 us -> none  [shards(): data_all = lax.all_gather(data_vec, 'stripe', axis=2, tiled=True)]
    dot_general x12 -> x0, matrix products: 23 us -> none  [the longest x1 5.66 us: shards(): jnp.einsum('kcsp,kcnp->kns', kernel, pair_real, preferred_element_type=jn...]
    pallas_call x0 -> x6, Pallas kernels: none -> 19.7 us  [call(): pl.pallas_call(body, out_shape=out_shape, in_specs=list(specs), out_specs...]
    unnamed x23 -> x0, local copies, waits for them, and re-layouts: 7.1 us -> none
  transfers between devices with their start and end apart: 3 -> 0, of which waited for: 3 -> 0; matrix products, arithmetic and copies ran while one was open for 0% -> 0% of each run, Pallas kernels for 0% -> 0%
where the time goes in v1:
time: 91.3 us; the launch traced here: 90.8 us
  blocking collectives  71.1 us (78%)
  Pallas kernels  19.7 us (22%)
    all_to_all x5, blocking collectives, exchange(): return lax.all_to_all(x, axis, 0, 0, tiled=True)  71.1 us
    pallas_call x6, Pallas kernels, call(): pl.pallas_call(body, out_shape=out_shape, in_specs=list(specs), out_specs...  19.7 us

profile of v1, /device:TPU:1, one launch (start us, length us, event | category | flops | bytes accessed | tf_op | source)
XLA Modules:
  0.0 90.8 jit_solution(10011024577141013641)
XLA Ops:
  0.0 1.4 %shard_map.91 = f32[128,128]{1,0:T(8,128)} custom-call(f32[4,2,64]{2,1,0:T(2,128)} %data_ref.3), custom_call_target="tpu_custom_call" | custom-call | tf_op jit(solution)/shard_map/pallas_call | solution.py:26
  1.4 22.3 %all_to_all.25 = f32[32,4,128]{2,1,0:T(4,128)} all-to-all(f32[32,4,128]{2,1,0:T(4,128)} %bitcast.11), channel_id=1, replica_groups=mesh['tm'=32,'stripe'=8] {'tm'}, dimensions={0} | all-to-all | bytes 131072 | tf_op jit(solution)/shard_map/all_to_all | solution.py:180
  23.6 1.7 %shard_map.92 = bf16[8,8,128]{2,1,0:T(8,128)(2,1)} custom-call(f32[128,128]{1,0:T(8,128)} %bitcast.9, f32[32,8,128]{2,1,0:T(8,128)} %constant.8.clone.table_ref), custom_call_target="tpu_custom_call" | custom-call | tf_op jit(solution)/shard_map/pallas_call | solution.py:26
  25.3 9.4 %all_to_all.26.gathered_ref = bf16[8,8,128]{2,1,0:T(8,128)(2,1)} all-to-all(bf16[8,8,128]{2,1,0:T(8,128)(2,1)} %shard_map.92), channel_id=1, replica_groups=mesh['tm'=32,'stripe'=8] {'stripe'}, dimensions={0} | all-to-all | bytes 32768 | tf_op jit(solution)/shard_map/all_to_all | solution.py:180
  34.7 5.8 %shard_map.93 = f32[8,16,1024]{2,1,0:T(8,128)} custom-call(bf16[8,8,128]{2,1,0:T(8,128)(2,1)} %all_to_all.26.gathered_ref, bf16[4,2,512,1024]{3,2,1,0:T(8,128)(2,1)} %kernel_ref.3, f32[4]{0:T(128)} %scale_ref.1, f32[128,128]{1,0:T(8,128)} %constant.11.clone.column_ref), custom_call_target="tpu_custom_call" | custom-call | tf_op jit(solution)/shard_map/pallas_call | solution.py:26
  40.5 11.6 %all_to_all.27 = f32[8,16,1024]{2,1,0:T(8,128)} all-to-all(f32[8,16,1024]{2,1,0:T(8,128)} %shard_map.93), channel_id=1, replica_groups=mesh['tm'=32,'stripe'=8] {'stripe'}, dimensions={0} | all-to-all | bytes 1048576 | tf_op jit(solution)/shard_map/all_to_all | solution.py:180
  52.1 7.5 %shard_map.94 = f32[8,8,128]{2,1,0:T(8,128)} custom-call(f32[128,1024]{1,0:T(8,128)} %bitcast.7, bf16[4,2,512,1024]{3,2,1,0:T(8,128)(2,1)} %kernel_ref.3, f32[64,128]{1,0:T(8,128)} %bitcast.12, f32[128,128]{1,0:T(8,128)} %constant.10.clone.forward_ref, f32[128,128]{1,0:T(8,128)} %constant.9.clone.backward_ref, f32[128,128]{1,0:T(8,128)} %constant.11.clone.column_ref), custom_call_target="tpu_custom_call" | custom-call | tf_op jit(solution)/shard_map/pallas_call | solution.py:26
  59.6 9.0 %all_to_all.28.images_ref = f32[8,8,128]{2,1,0:T(8,128)} all-to-all(f32[8,8,128]{2,1,0:T(8,128)} %shard_map.94), channel_id=1, replica_groups=mesh['tm'=32,'stripe'=8] {'stripe'}, dimensions={0} | all-to-all | bytes 65536 | tf_op jit(solution)/shard_map/all_to_all | solution.py:180
  68.6 1.8 %shard_map.95 = f32[128,128]{1,0:T(8,128)} custom-call(f32[8,8,128]{2,1,0:T(8,128)} %all_to_all.28.images_ref, f32[32,8,128]{2,1,0:T(8,128)} %constant.8.clone.table_ref), custom_call_target="tpu_custom_call" | custom-call | tf_op jit(solution)/shard_map/pallas_call | solution.py:26
  70.4 18.8 %all_to_all.29 = f32[32,4,128]{2,1,0:T(4,128)} all-to-all(f32[32,4,128]{2,1,0:T(4,128)} %bitcast.8), channel_id=1, replica_groups=mesh['tm'=32,'stripe'=8] {'tm'}, dimensions={0} | all-to-all | bytes 131072 | tf_op jit(solution)/shard_map/all_to_all | solution.py:180
  89.2 1.6 %shard_map.96 = f32[4,2,64]{2,1,0:T(2,128)} custom-call(f32[128,128]{1,0:T(8,128)} %bitcast.10, f32[4,2,64]{2,1,0:T(2,128)} %data_ref.3, f32[1,64]{1,0:T(1,128)} %bitcast.13), custom_call_target="tpu_custom_call" | custom-call | tf_op jit(solution)/shard_map/pallas_call | solution.py:26

commit v2 on v1

--- a/solution.py
+++ b/solution.py
@@ -22,13 +22,17 @@
     return pl.BlockSpec(memory_space=pltpu.SMEM)
 
 
-def call(body, out_shape, operands, specs, scratch=()):
+def call(body, out_shape, operands, specs, scratch=(), limit=4 << 20, hint=1e6):
     return pl.pallas_call(
         body,
         out_shape=out_shape,
         in_specs=list(specs),
         out_specs=whole(),
         scratch_shapes=list(scratch),
+        cost_estimate=pl.CostEstimate(
+            flops=int(hint), transcendentals=0, bytes_accessed=100_000
+        ),
+        compiler_params=pltpu.CompilerParams(vmem_limit_bytes=limit),
     )(*operands)
 
 
@@ -189,13 +193,20 @@
     columns = sine_matrix(64)
     column = jnp.asarray(np.kron(np.eye(2), columns).astype(np.float32))
 
-    spread = call(spread_body, jax.ShapeDtypeStruct((128, 128), f32), (data_vec,), (whole(),))
+    spread = call(
+        spread_body,
+        jax.ShapeDtypeStruct((128, 128), f32),
+        (data_vec,),
+        (whole(),),
+        hint=2e10,
+    )
     by_time = exchange(spread.reshape(32, 4, 128), "tm").reshape(128, 128)
     spectra = call(
         spectra_body,
         jax.ShapeDtypeStruct((8, 8, 128), bf16),
         (by_time, table),
         (whole(), whole()),
+        hint=2e10,
     )
     gathered = exchange(spectra, "stripe")
     grids = call(
@@ -204,6 +215,7 @@
         (gathered, kernel, time_spectrum, column),
         (whole(), whole(), scalars(), whole()),
         (pltpu.VMEM((128, 128), f32),),
+        limit=20 << 20,
     )
     grids = exchange(grids, "stripe").reshape(128, 1024)
     images = call(
@@ -212,6 +224,7 @@
         (grids, kernel, prior_spectrum.T, forward, backward, column),
         (whole(),) * 6,
         (pltpu.VMEM((128, 128), f32),),
+        limit=20 << 20,
     )
     images = exchange(images, "stripe")
     sums = call(

time: 91.3 us -> 74.3 us (0.81)
  Pallas kernels: 19.7 us -> 6.76 us
  blocking collectives: 71.1 us -> 66.4 us
    pallas_call x6, Pallas kernels: 19.7 us -> 6.76 us  [call(): pl.pallas_call(body, out_shape=out_shape, in_specs=list(specs), out_specs...]
    all_to_all x5, blocking collectives: 71.1 us -> 66.4 us  [exchange(): return lax.all_to_all(x, axis, 0, 0, tiled=True)]
where the time goes in v2:
time: 74.3 us; the launch traced here: 74 us
  blocking collectives  66.4 us (89%)
  Pallas kernels  6.76 us (9%)
  local copies, waits for them, and re-layouts  0.76 us (1%)
    all_to_all x5, blocking collectives, exchange(): return lax.all_to_all(x, axis, 0, 0, tiled=True)  66.4 us
    pallas_call x6, Pallas kernels, call(): pl.pallas_call(body, out_shape=out_shape, in_specs=list(specs), out_specs...  6.76 us

profile of v2, /device:TPU:1, one launch (start us, length us, event | category | flops | bytes accessed | tf_op | source)
XLA Modules:
  0.0 74.0 jit_solution(5166811056723484110)
XLA Ops:
  0.0 0.0 copy-start.1
  0.0 0.0 copy-start.5
  0.0 0.7 copy-done.5
  0.7 0.0 slice-start
  0.7 0.1 shard_map.91
  0.8 0.0 slice-start.1
  0.8 22.2 %all_to_all.25 = f32[32,4,128]{2,1,0:T(4,128)S(1)} all-to-all(f32[32,4,128]{2,1,0:T(4,128)S(1)} %bitcast.13), channel_id=1, replica_groups=mesh['tm'=32,'stripe'=8] {'tm'}, dimensions={0} | all-to-all | bytes 131072 | tf_op jit(solution)/shard_map/all_to_all | solution.py:184
  23.0 0.0 copy-done.1
  23.0 0.0 copy-start
  23.0 0.0 copy-start.6
  23.0 0.2 shard_map.92
  23.2 0.0 copy-start.2
  23.2 0.0 copy-start.3
  23.2 0.0 copy-start.4
  23.2 9.2 %all_to_all.26.gathered_ref = bf16[8,8,128]{2,1,0:T(8,128)(2,1)S(1)} all-to-all(bf16[8,8,128]{2,1,0:T(8,128)(2,1)S(1)} %shard_map.92), channel_id=1, replica_groups=mesh['tm'=32,'stripe'=8] {'stripe'}, dimensions={0} | all-to-all | bytes 32768 | tf_op jit(solution)/shard_map/all_to_all | solution.py:184
  32.4 0.0 slice-done
  32.4 0.0 slice-done.1
  32.4 0.0 copy-done
  32.4 0.0 copy-done.6
  32.4 0.0 copy-start.7
  32.4 2.1 %shard_map.93 = f32[8,16,1024]{2,1,0:T(8,128)S(1)} custom-call(bf16[8,8,128]{2,1,0:T(8,128)(2,1)S(1)} %all_to_all.26.gathered_ref, bf16[4,2,512,1024]{3,2,1,0:T(8,128)(2,1)S(1)} %bitcast.8, f32[4]{0:T(128)S(1)} %copy-done.6, f32[128,128]{1,0:T(8,128)S(1)} %copy-done), custom_call_target="tpu_custom_call" | custom-call | flops 1000000 | bytes 100000 | tf_op jit(solution)/shard_map/pallas_call | solution.py:26
  34.6 9.9 %all_to_all.27 = f32[8,16,1024]{2,1,0:T(8,128)S(1)} all-to-all(f32[8,16,1024]{2,1,0:T(8,128)S(1)} %shard_map.93), channel_id=1, replica_groups=mesh['tm'=32,'stripe'=8] {'stripe'}, dimensions={0} | all-to-all | bytes 1048576 | tf_op jit(solution)/shard_map/all_to_all | solution.py:184
  44.5 0.0 copy-done.2
  44.5 0.0 copy-done.3
  44.5 0.0 copy-done.4
  44.5 3.4 %shard_map.94 = f32[8,8,128]{2,1,0:T(8,128)S(1)} custom-call(f32[128,1024]{1,0:T(8,128)S(1)} %bitcast.9, bf16[4,2,512,1024]{3,2,1,0:T(8,128)(2,1)S(1)} %bitcast.8, f32[64,128]{1,0:T(8,128)S(1)} %bitcast.14, f32[128,128]{1,0:T(8,128)S(1)} %copy-done.2, f32[128,128]{1,0:T(8,128)S(1)} %copy-done.3, f32[128,128]{1,0:T(8,128)S(1)} %copy-done), custom_call_target="tpu_custom_call" | custom-call | flops 1000000 | bytes 100000 | tf_op jit(solution)/shard_map/pallas_call | solution.py:26
  47.9 7.5 %all_to_all.28.images_ref = f32[8,8,128]{2,1,0:T(8,128)S(1)} all-to-all(f32[8,8,128]{2,1,0:T(8,128)S(1)} %shard_map.94), channel_id=1, replica_groups=mesh['tm'=32,'stripe'=8] {'stripe'}, dimensions={0} | all-to-all | bytes 65536 | tf_op jit(solution)/shard_map/all_to_all | solution.py:184
  55.4 0.3 shard_map.95
  55.6 17.6 %all_to_all.29 = f32[32,4,128]{2,1,0:T(4,128)S(1)} all-to-all(f32[32,4,128]{2,1,0:T(4,128)S(1)} %bitcast.10), channel_id=1, replica_groups=mesh['tm'=32,'stripe'=8] {'tm'}, dimensions={0} | all-to-all | bytes 131072 | tf_op jit(solution)/shard_map/all_to_all | solution.py:184
  73.3 0.0 copy-done.7
  73.3 0.7 %shard_map.96 = f32[4,2,64]{2,1,0:T(2,128)} custom-call(f32[128,128]{1,0:T(8,128)S(1)} %bitcast.11, f32[4,2,64]{2,1,0:T(2,128)S(1)} %copy-done.5, f32[1,64]{1,0:T(1,128)S(1)} %bitcast.15), custom_call_target="tpu_custom_call" | custom-call | flops 1000000 | bytes 100000 | tf_op jit(solution)/shard_map/pallas_call | solution.py:26
  (1 shorter events, 0.0 us)
Async XLA Ops:
  0.0 23.0 %copy-start.1 = (f32[32,8,128]{2,1,0:T(8,128)S(1)}, f32[32,8,128]{2,1,0:T(8,128)}, u32[]{:S(2)}) copy-start(f32[32,8,128]{2,1,0:T(8,128)} %constant.8.clone.table_ref) | copy-start | bytes 393220
  0.0 0.7 copy-start.5
  0.7 31.7 %slice-start = ((s8[8388608]{0:T(1024)(128)(4,1)}), s8[4194304]{0:T(1024)(128)(4,1)S(1)}, s32[]{:S(2)}) async-start(s8[8388608]{0:T(1024)(128)(4,1)} %bitcast.7), calls=%async_computation.5 | async-start | bytes 8388608
  0.8 31.6 %slice-start.1 = ((s8[8388608]{0:T(1024)(128)(4,1)}), s8[4194304]{0:T(1024)(128)(4,1)S(1)}, s32[]{:S(2)}) async-start(s8[8388608]{0:T(1024)(128)(4,1)} %bitcast.7), calls=%async_computation.6 | async-start | bytes 8388608
  23.0 9.4 %copy-start = (f32[128,128]{1,0:T(8,128)S(1)}, f32[128,128]{1,0:T(8,128)}, u32[]{:S(2)}) copy-start(f32[128,128]{1,0:T(8,128)} %constant.11.clone.column_ref) | copy-start | bytes 196612
  23.0 9.4 %copy-start.6 = (f32[4]{0:T(128)S(1)}, f32[4]{0:T(128)}, u32[]{:S(2)}) copy-start(f32[4]{0:T(128)} %scale_ref.1) | copy-start | bytes 52
  23.2 21.3 %copy-start.2 = (f32[128,128]{1,0:T(8,128)S(1)}, f32[128,128]{1,0:T(8,128)}, u32[]{:S(2)}) copy-start(f32[128,128]{1,0:T(8,128)} %constant.10.clone.forward_ref) | copy-start | bytes 196612
  23.2 21.3 %copy-start.3 = (f32[128,128]{1,0:T(8,128)S(1)}, f32[128,128]{1,0:T(8,128)}, u32[]{:S(2)}) copy-start(f32[128,128]{1,0:T(8,128)} %constant.9.clone.backward_ref) | copy-start | bytes 196612
  23.2 21.3 %copy-start.4 = (f32[128,64]{0,1:T(8,128)S(1)}, f32[128,64]{0,1:T(8,128)}, u32[]{:S(2)}) copy-start(f32[128,64]{0,1:T(8,128)} %param.12) | copy-start | bytes 98308
  32.4 40.8 %copy-start.7 = (f32[64]{0:T(128)S(1)}, f32[64]{0:T(128)}, u32[]{:S(2)}) copy-start(f32[64]{0:T(128)} %param.13) | copy-start | bytes 772

commit v3 on v2

--- a/solution.py
+++ b/solution.py
@@ -42,12 +42,12 @@
     )
 
 
-def fourier_table(blocks):
+def fourier_table(halves, blocks):
     steps = np.arange(128)
     angles = np.outer(steps, steps) % 256 * (math.pi / 128)
     pair = np.stack([np.cos(angles), -np.sin(angles)]) / math.sqrt(128)
-    pair = pair.reshape(2, blocks, 128 // blocks, 128).transpose(1, 0, 2, 3)
-    return pair.reshape(blocks, 2 * (128 // blocks), 128).astype(np.float32)
+    pair = pair.reshape(2, halves, blocks, 4, halves, 64).transpose(4, 2, 1, 0, 3, 5)
+    return pair.reshape(halves, blocks, halves * 8, 64).astype(np.float32)
 
 
 def sine_matrix(length):
@@ -72,25 +72,49 @@
     return low, high
 
 
+def split(x):
+    high = x.astype(bf16)
+    return high, (x - high.astype(f32)).astype(bf16)
+
+
+def split_table(x):
+    high = x.astype(np.float32).astype(bf16)
+    return high, (x - high.astype(np.float64)).astype(np.float32).astype(bf16)
+
+
+def column_transform(x, high_ref, low_ref):
+    high, low = split(x)
+    return (
+        mm(high, high_ref[...], precision=None)
+        + mm(low, high_ref[...], precision=None)
+        + mm(high, low_ref[...], precision=None)
+    )
+
+
 def spread_body(data_ref, out_ref):
     flat = jnp.concatenate([data_ref[:, 0, :], data_ref[:, 1, :]], axis=1)
     two = jnp.concatenate([flat, flat], axis=0)
-    for r in range(16):
+    for r in range(8):
         out_ref[r * 8 : r * 8 + 8, :] = two
 
 
+def block_of_table(table_ref):
+    tm = lax.axis_index("tm")
+    return table_ref[tm // 16, tm % 16]
+
+
 def spectra_body(data_ref, table_ref, out_ref):
-    tm = lax.axis_index("tm")
-    spectra = mm(table_ref[tm], data_ref[...]).astype(bf16)
-    for r in range(8):
-        out_ref[r] = spectra
-
-
-def adjoint_body(gathered_ref, kernel_ref, scale_ref, column_ref, out_ref, grid_ref):
+    spectra = mm(block_of_table(table_ref), data_ref[...])
+    for half in range(2):
+        for r in range(8):
+            out_ref[half, r] = spectra[half * 8 : half * 8 + 8, :]
+
+
+def adjoint_body(gathered_ref, kernel_ref, scale_ref, high_ref, low_ref, out_ref, grid_ref):
     parts = [[], []]
     for j in range(4):
-        first = gathered_ref[2 * j].astype(f32)
-        second = gathered_ref[2 * j + 1].astype(f32)
+        first = gathered_ref[0, 2 * j] + gathered_ref[1, 2 * j]
+        second = gathered_ref[0, 2 * j + 1] + gathered_ref[1, 2 * j + 1]
         low, high = swap_halves(first, second)
         parts[0].append(low)
         parts[1].append(high)
@@ -114,32 +138,34 @@
     )
     total = total * scale
     stack = jnp.concatenate([total[:, c * 128 : c * 128 + 128] for c in range(8)], axis=0)
-    grid_ref[...] = mm(stack, column_ref[...])
+    grid_ref[...] = column_transform(stack, high_ref, low_ref)
     for m in range(8):
         first = grid_ref[pl.ds(2 * m, 8, stride=16), :]
         second = grid_ref[pl.ds(2 * m + 1, 8, stride=16), :]
-        low, high = swap_halves(first, second)
+        tile = jnp.concatenate(swap_halves(first, second), axis=0).astype(bf16)
         for r in range(8):
-            out_ref[r, 0:8, m * 128 : m * 128 + 128] = low
-            out_ref[r, 8:16, m * 128 : m * 128 + 128] = high
+            out_ref[r, :, m * 128 : m * 128 + 128] = tile
 
 
 def images_body(
-    grids_ref, kernel_ref, prior_ref, forward_ref, backward_ref, column_ref, out_ref, grid_ref
+    grids_ref, kernel_ref, prior_ref, forward_ref, backward_ref, high_ref, low_ref, out_ref, grid_ref
 ):
     stripe = lax.axis_index("stripe")
-    modes = mm(forward_ref[...], grids_ref[...])
+    grids = grids_ref[...]
+    modes = mm(forward_ref[...], jnp.concatenate([grids, grids], axis=0), precision=None)
     prior = prior_ref[...].T
     prior = jnp.concatenate([prior, prior], axis=1)
     modes = modes * jnp.concatenate([prior] * 8, axis=1)
-    back = mm(backward_ref[pl.ds(stripe * 16, 16), :], modes)
+    modes = jnp.concatenate(split(modes), axis=0)
+    back = mm(backward_ref[stripe], modes, precision=None)
+    back = back[0:16, :] + back[16:32, :]
     for m in range(8):
         first, second = swap_halves(
             back[0:8, m * 128 : m * 128 + 128], back[8:16, m * 128 : m * 128 + 128]
         )
         grid_ref[pl.ds(2 * m, 8, stride=16), :] = first
         grid_ref[pl.ds(2 * m + 1, 8, stride=16), :] = second
-    smooth = mm(grid_ref[...], column_ref[...])
+    smooth = column_transform(grid_ref[...], high_ref, low_ref)
     smooth = jnp.concatenate([smooth[c * 16 : c * 16 + 16, :] for c in range(8)], axis=1)
     sub = lax.broadcasted_iota(jnp.int32, (8, 1024), 0)
     turned = []
@@ -158,21 +184,25 @@
         low, high = swap_halves(
             total[0:8, j * 128 : j * 128 + 128], total[8:16, j * 128 : j * 128 + 128]
         )
-        out_ref[2 * j] = low
-        out_ref[2 * j + 1] = high
+        for half in range(2):
+            out_ref[half, 2 * j] = low
+            out_ref[half, 2 * j + 1] = high
 
 
 def times_body(images_ref, table_ref, out_ref):
-    tm = lax.axis_index("tm")
-    total = images_ref[0]
-    for r in range(1, 8):
-        total = total + images_ref[r]
-    out_ref[...] = mm(table_ref[tm], total, ((0,), (0,)))
+    halves = []
+    for half in range(2):
+        total = images_ref[half, 0]
+        for r in range(1, 8):
+            total = total + images_ref[half, r]
+        halves.append(total)
+    images = jnp.concatenate(halves, axis=0)
+    out_ref[...] = mm(block_of_table(table_ref), images, ((0,), (0,)))
 
 
 def finish_body(sums_ref, data_ref, noise_ref, out_ref):
     total = sums_ref[0:8, :]
-    for r in range(1, 16):
+    for r in range(1, 8):
         total = total + sums_ref[r * 8 : r * 8 + 8, :]
     total = total[0:4, :] + total[4:8, :]
     noise = noise_ref[...]
@@ -180,57 +210,68 @@
     out_ref[:, 1, :] = total[:, 64:128] + noise * data_ref[:, 1, :]
 
 
-def exchange(x, axis):
-    return lax.all_to_all(x, axis, 0, 0, tiled=True)
+def exchange(x, axis, groups=None):
+    return lax.all_to_all(x, axis, 0, 0, tiled=True, axis_index_groups=groups)
 
 
 def shards(data_vec, kernel, time_spectrum, prior_spectrum, noise_var):
-    table = jnp.asarray(fourier_table(32))
+    table = jnp.asarray(fourier_table(2, 16))
     rows = sine_matrix(128)
     order = row_order()
-    backward = jnp.asarray(rows[order].astype(np.float32))
-    forward = jnp.asarray(rows[:, order].astype(np.float32))
-    columns = sine_matrix(64)
-    column = jnp.asarray(np.kron(np.eye(2), columns).astype(np.float32))
+    forward = jnp.asarray(np.concatenate(split_table(rows[:, order]), axis=1))
+    high, low = split_table(rows[order].reshape(8, 16, 128))
+    upper = np.concatenate([high, high], axis=2)
+    lower = np.concatenate([low, np.zeros_like(low)], axis=2)
+    backward = jnp.asarray(np.concatenate([upper, lower], axis=1))
+    columns = [jnp.asarray(t) for t in split_table(np.kron(np.eye(2), sine_matrix(64)))]
+
+    first = [[half * 16 + block for block in range(16)] for half in range(2)]
+    second = [
+        [(half * 16 + block) * 8 + stripe for half in range(2) for stripe in range(8)]
+        for block in range(16)
+    ]
 
     spread = call(
         spread_body,
-        jax.ShapeDtypeStruct((128, 128), f32),
+        jax.ShapeDtypeStruct((64, 128), f32),
         (data_vec,),
         (whole(),),
         hint=2e10,
     )
-    by_time = exchange(spread.reshape(32, 4, 128), "tm").reshape(128, 128)
+    by_time = exchange(spread.reshape(16, 4, 128), "tm", first).reshape(64, 128)
     spectra = call(
         spectra_body,
-        jax.ShapeDtypeStruct((8, 8, 128), bf16),
+        jax.ShapeDtypeStruct((2, 8, 8, 128), f32),
         (by_time, table),
         (whole(), whole()),
         hint=2e10,
     )
-    gathered = exchange(spectra, "stripe")
+    gathered = exchange(spectra.reshape(16, 8, 128), ("tm", "stripe"), second)
     grids = call(
         adjoint_body,
-        jax.ShapeDtypeStruct((8, 16, 1024), f32),
-        (gathered, kernel, time_spectrum, column),
-        (whole(), whole(), scalars(), whole()),
+        jax.ShapeDtypeStruct((8, 16, 1024), bf16),
+        (gathered.reshape(2, 8, 8, 128), kernel, time_spectrum, *columns),
+        (whole(), whole(), scalars(), whole(), whole()),
         (pltpu.VMEM((128, 128), f32),),
         limit=20 << 20,
     )
     grids = exchange(grids, "stripe").reshape(128, 1024)
     images = call(
         images_body,
-        jax.ShapeDtypeStruct((8, 8, 128), f32),
-        (grids, kernel, prior_spectrum.T, forward, backward, column),
-        (whole(),) * 6,
+        jax.ShapeDtypeStruct((2, 8, 8, 128), f32),
+        (grids, kernel, prior_spectrum.T, forward, backward, *columns),
+        (whole(),) * 7,
         (pltpu.VMEM((128, 128), f32),),
         limit=20 << 20,
     )
-    images = exchange(images, "stripe")
+    images = exchange(images.reshape(16, 8, 128), ("tm", "stripe"), second)
     sums = call(
-        times_body, jax.ShapeDtypeStruct((128, 128), f32), (images, table), (whole(), whole())
-    )
-    sums = exchange(sums.reshape(32, 4, 128), "tm").reshape(128, 128)
+        times_body,
+        jax.ShapeDtypeStruct((64, 128), f32),
+        (images.reshape(2, 8, 8, 128), table),
+        (whole(), whole()),
+    )
+    sums = exchange(sums.reshape(16, 4, 128), "tm", first).reshape(64, 128)
     return call(
         finish_body,
         jax.ShapeDtypeStruct((4, 2, 64), f32),

time: 74.3 us -> 70.8 us (0.953)
  blocking collectives: 66.4 us -> 63.4 us
    all_to_all x5, blocking collectives: 66.4 us -> 63.4 us  [exchange(): return lax.all_to_all(x, axis, 0, 0, tiled=True, axis_index_groups=groups)]
where the time goes in v3:
time: 70.8 us; the launch traced here: 70.5 us
  blocking collectives  63.4 us (90%)
  Pallas kernels  6.21 us (9%)
  local copies, waits for them, and re-layouts  0.79 us (1%)
    all_to_all x5, blocking collectives, exchange(): return lax.all_to_all(x, axis, 0, 0, tiled=True, axis_index_groups=groups)  63.4 us
    pallas_call x6, Pallas kernels, call(): pl.pallas_call(body, out_shape=out_shape, in_specs=list(specs), out_specs...  6.21 us

profile of v3, /device:TPU:1, one launch (start us, length us, event | category | flops | bytes accessed | tf_op | source)
XLA Modules:
  0.0 70.5 jit_solution(2766880509772234284)
XLA Ops:
  0.0 0.0 copy-start
  0.0 0.0 copy-start.6
  0.0 0.7 %copy-done.6 = f32[4,2,64]{2,1,0:T(2,128)S(1)} copy-done((f32[4,2,64]{2,1,0:T(2,128)S(1)}, f32[4,2,64]{2,1,0:T(2,128)}, u32[]{:S(2)}) %copy-start.6) | copy-done | bytes 2072
  0.7 0.0 slice-start
  0.7 0.1 shard_map.100
  0.8 17.4 %all_to_all.25 = f32[16,4,128]{2,1,0:T(4,128)S(1)} all-to-all(f32[16,4,128]{2,1,0:T(4,128)S(1)} %bitcast.22), channel_id=1, replica_groups={{0,8,16,24,32,40,48,56,64,72,80,88,96,104,112,120},{128,136,144,152,160..., dimensions={0} | all-to-all | bytes 65536 | tf_op jit(solution)/shard_map/all_to_all | solution.py:214
  18.2 0.0 copy-done
  18.2 0.0 slice-start.1
  18.2 0.0 copy-start.8
  18.2 0.2 shard_map.101
  18.4 0.0 copy-start.4
  18.4 0.0 copy-start.5
  18.4 13.3 %all_to_all.26 = f32[16,8,128]{2,1,0:T(8,128)S(1)} all-to-all(f32[16,8,128]{2,1,0:T(8,128)S(1)} %bitcast.19), channel_id=1, replica_groups={{0,1,2,3,4,5,6,7,128,129,130,131,132,133,134,135},{8,9,10,11,12,13,14,1..., dimensions={0} | all-to-all | bytes 131072 | tf_op jit(solution)/shard_map/all_to_all | solution.py:214
  31.8 0.0 slice-done
  31.8 0.0 slice-done.1
  31.8 0.0 copy-done.2
  31.8 0.0 copy-done.3
  31.8 0.0 copy-done.8
  31.8 0.0 copy-start.7
  31.8 0.0 copy-start.9
  31.8 2.1 %shard_map.102 = bf16[8,16,1024]{2,1,0:T(8,128)(2,1)S(1)} custom-call(f32[2,8,8,128]{3,2,1,0:T(8,128)S(1)} %bitcast.15, bf16[4,2,512,1024]{3,2,1,0:T(8,128)(2,1)S(1)} %bitcast.12, f32[4]{0:T(128)S(1)} %copy-done.8, bf16[128,128]{1,0:T(8,128)(2,1)S(1)} %copy-done.3, bf16[128,128]{1,0:T(8,128)(2,1)S(1)} %copy-done.2), custom_call_target="tpu_custom_call" | custom-call | flops 1000000 | bytes 100000 | tf_op jit(solution)/shard_map/pallas_call | solution.py:26
  33.9 8.6 %all_to_all.27 = bf16[8,16,1024]{2,1,0:T(8,128)(2,1)S(1)} all-to-all(bf16[8,16,1024]{2,1,0:T(8,128)(2,1)S(1)} %shard_map.102), channel_id=1, replica_groups=mesh['tm'=32,'stripe'=8] {'stripe'}, dimensions={0} | all-to-all | bytes 524288 | tf_op jit(solution)/shard_map/all_to_all | solution.py:214
  42.5 0.0 copy-done.1
  42.5 0.0 copy-done.4
  42.5 0.0 copy-done.5
  42.5 2.9 %shard_map.103 = f32[2,8,8,128]{3,2,1,0:T(8,128)S(1)} custom-call(bf16[128,1024]{1,0:T(8,128)(2,1)S(1)} %bitcast.13, bf16[4,2,512,1024]{3,2,1,0:T(8,128)(2,1)S(1)} %bitcast.12, f32[64,128]{1,0:T(8,128)S(1)} %bitcast.20, bf16[128,256]{1,0:T(8,128)(2,1)S(1)} %copy-done.4, bf16[8,32,256]{2,1,0:T(8,128)(2,1)S(1)} %copy-done.1, bf16[128,128]{1,0:T(8,128)(2,1)S(1)} %copy-done.3, ...), custom_call_target="tpu_custom_call" | custom-call | flops 1000000 | bytes 100000 | tf_op jit(solution)/shard_map/pallas_call | solution.py:26
  45.4 10.1 %all_to_all.28 = f32[16,8,128]{2,1,0:T(8,128)S(1)} all-to-all(f32[16,8,128]{2,1,0:T(8,128)S(1)} %bitcast.14), channel_id=1, replica_groups={{0,1,2,3,4,5,6,7,128,129,130,131,132,133,134,135},{8,9,10,11,12,13,14,1..., dimensions={0} | all-to-all | bytes 131072 | tf_op jit(solution)/shard_map/all_to_all | solution.py:214
  55.5 0.2 shard_map.104
  55.7 14.0 %all_to_all.29 = f32[16,4,128]{2,1,0:T(4,128)S(1)} all-to-all(f32[16,4,128]{2,1,0:T(4,128)S(1)} %bitcast.18), channel_id=1, replica_groups={{0,8,16,24,32,40,48,56,64,72,80,88,96,104,112,120},{128,136,144,152,160..., dimensions={0} | all-to-all | bytes 65536 | tf_op jit(solution)/shard_map/all_to_all | solution.py:214
  69.7 0.0 copy-done.7
  69.7 0.0 copy-done.9
  69.7 0.7 %shard_map.105 = f32[4,2,64]{2,1,0:T(2,128)} custom-call(f32[64,128]{1,0:T(8,128)S(1)} %bitcast.17, f32[4,2,64]{2,1,0:T(2,128)S(1)} %copy-done.7, f32[1,64]{1,0:T(1,128)S(1)} %bitcast.23), custom_call_target="tpu_custom_call" | custom-call | flops 1000000 | bytes 100000 | tf_op jit(solution)/shard_map/pallas_call | solution.py:26
  (4 shorter events, 0.0 us)
Async XLA Ops:
  0.0 18.2 %copy-start = (f32[2,16,16,64]{3,2,1,0:T(8,128)S(1)}, f32[2,16,16,64]{3,2,1,0:T(8,128)}, u32[]{:S(2)}) copy-start(f32[2,16,16,64]{3,2,1,0:T(8,128)} %constant.10.clone.table_ref) | copy-start | bytes 393220
  0.0 0.7 %copy-start.6 = (f32[4,2,64]{2,1,0:T(2,128)S(1)}, f32[4,2,64]{2,1,0:T(2,128)}, u32[]{:S(2)}) copy-start(f32[4,2,64]{2,1,0:T(2,128)} %data_ref.3) | copy-start | bytes 6148
  0.7 31.0 %slice-start = ((s8[8388608]{0:T(1024)(128)(4,1)}), s8[4194304]{0:T(1024)(128)(4,1)S(1)}, s32[]{:S(2)}) async-start(s8[8388608]{0:T(1024)(128)(4,1)} %bitcast.11), calls=%async_computation.5 | async-start | bytes 8388608
  18.2 13.5 %slice-start.1 = ((s8[8388608]{0:T(1024)(128)(4,1)}), s8[4194304]{0:T(1024)(128)(4,1)S(1)}, s32[]{:S(2)}) async-start(s8[8388608]{0:T(1024)(128)(4,1)} %bitcast.11), calls=%async_computation.6 | async-start | bytes 8388608
  18.2 13.5 %copy-start.2 = (bf16[128,128]{1,0:T(8,128)(2,1)S(1)}, bf16[128,128]{1,0:T(8,128)(2,1)}, u32[]{:S(2)}) copy-start(bf16[128,128]{1,0:T(8,128)(2,1)} %constant.14.clone.low_ref) | copy-start | bytes 98308
  18.2 13.6 %copy-start.3 = (bf16[128,128]{1,0:T(8,128)(2,1)S(1)}, bf16[128,128]{1,0:T(8,128)(2,1)}, u32[]{:S(2)}) copy-start(bf16[128,128]{1,0:T(8,128)(2,1)} %constant.13.clone.high_ref) | copy-start | bytes 98308
  18.2 13.6 %copy-start.8 = (f32[4]{0:T(128)S(1)}, f32[4]{0:T(128)}, u32[]{:S(2)}) copy-start(f32[4]{0:T(128)} %scale_ref.1) | copy-start | bytes 52
  18.4 24.1 %copy-start.1 = (bf16[8,32,256]{2,1,0:T(8,128)(2,1)S(1)}, bf16[8,32,256]{2,1,0:T(8,128)(2,1)}, u32[]{:S(2)}) copy-start(bf16[8,32,256]{2,1,0:T(8,128)(2,1)} %constant.12.clone.backward_ref) | copy-start | bytes 393220
  18.4 24.1 %copy-start.4 = (bf16[128,256]{1,0:T(8,128)(2,1)S(1)}, bf16[128,256]{1,0:T(8,128)(2,1)}, u32[]{:S(2)}) copy-start(bf16[128,256]{1,0:T(8,128)(2,1)} %constant.11.clone.forward_ref) | copy-start | bytes 196612
  18.4 24.1 %copy-start.5 = (f32[128,64]{0,1:T(8,128)S(1)}, f32[128,64]{0,1:T(8,128)}, u32[]{:S(2)}) copy-start(f32[128,64]{0,1:T(8,128)} %param.13) | copy-start | bytes 98308
  31.8 37.9 %copy-start.7 = (f32[4,2,64]{2,1,0:T(2,128)S(1)}, f32[4,2,64]{2,1,0:T(2,128)}, u32[]{:S(2)}) copy-start(f32[4,2,64]{2,1,0:T(2,128)} %data_ref.3) | copy-start | bytes 6148
  31.8 37.9 %copy-start.9 = (f32[64]{0:T(128)S(1)}, f32[64]{0:T(128)}, u32[]{:S(2)}) copy-start(f32[64]{0:T(128)} %param.14) | copy-start | bytes 772

commit v4 on v3

--- a/solution.py
+++ b/solution.py
@@ -48,6 +48,15 @@
     pair = np.stack([np.cos(angles), -np.sin(angles)]) / math.sqrt(128)
     pair = pair.reshape(2, halves, blocks, 4, halves, 64).transpose(4, 2, 1, 0, 3, 5)
     return pair.reshape(halves, blocks, halves * 8, 64).astype(np.float32)
+
+
+def inverse_table():
+    steps = np.arange(128)
+    angles = np.outer(steps, steps) % 256 * (math.pi / 128)
+    pair = np.stack([np.cos(angles), -np.sin(angles)]) / math.sqrt(128)
+    pair = pair.reshape(2, 2, 8, 2, 4, 2, 8, 2, 4)
+    pair = pair.transpose(2, 5, 7, 1, 3, 0, 4, 6, 8)
+    return pair.reshape(8, 4, 32, 32).astype(np.float32)
 
 
 def sine_matrix(length):
@@ -123,13 +132,13 @@
     turned = [jnp.where(sub < 4, pltpu.roll(r, 4, 0), -pltpu.roll(r, 4, 0)) for r in rows]
     straight = jnp.concatenate(rows, axis=0)
     turned = jnp.concatenate(turned, axis=0)
-    freq = lax.broadcasted_iota(jnp.int32, (16, 512), 0) % 4
+    both = jnp.concatenate([straight, turned], axis=1)
+    freq = lax.broadcasted_iota(jnp.int32, (16, 1024), 0) % 4
     total = None
     for k in range(4):
-        for c, source in enumerate((straight, turned)):
-            left = jnp.where(freq == k, source, 0.0).astype(bf16)
-            term = mm(left, kernel_ref[k, c], precision=None)
-            total = term if total is None else total + term
+        left = jnp.where(freq == k, both, 0.0).astype(bf16)
+        term = mm(left, kernel_ref[k].reshape(1024, 1024), precision=None)
+        total = term if total is None else total + term
     row = lax.broadcasted_iota(jnp.int32, (16, 1024), 0) % 4
     scale = jnp.where(
         row < 2,
@@ -167,42 +176,44 @@
         grid_ref[pl.ds(2 * m + 1, 8, stride=16), :] = second
     smooth = column_transform(grid_ref[...], high_ref, low_ref)
     smooth = jnp.concatenate([smooth[c * 16 : c * 16 + 16, :] for c in range(8)], axis=1)
-    sub = lax.broadcasted_iota(jnp.int32, (8, 1024), 0)
-    turned = []
+    left = smooth.astype(bf16)
+    products = mm(left, kernel_ref[...].reshape(4096, 1024), ((1,), (1,)), precision=None)
+    freq = lax.broadcasted_iota(jnp.int32, (16, 1024), 0) % 4
+    total = jnp.where(freq == 0, products[:, 0:1024], 0.0)
+    for k in range(1, 4):
+        total = jnp.where(freq == k, products[:, k * 1024 : k * 1024 + 1024], total)
+    sub = lax.broadcasted_iota(jnp.int32, (8, 512), 0)
+    rows = []
     for n in range(2):
-        moved = pltpu.roll(smooth[n * 8 : n * 8 + 8, :], 4, 0)
-        turned.append(jnp.where(sub < 4, -moved, moved))
-    turned = jnp.concatenate(turned, axis=0)
-    freq = lax.broadcasted_iota(jnp.int32, (16, 1024), 0) % 4
-    total = None
-    for k in range(4):
-        for c, source in enumerate((smooth, turned)):
-            left = jnp.where(freq == k, source, 0.0).astype(bf16)
-            term = mm(left, kernel_ref[k, c], ((1,), (1,)), precision=None)
-            total = term if total is None else total + term
+        moved = pltpu.roll(total[n * 8 : n * 8 + 8, 512:], 4, 0)
+        rows.append(total[n * 8 : n * 8 + 8, :512] + jnp.where(sub < 4, -moved, moved))
+    total = jnp.concatenate(rows, axis=0)
     for j in range(4):
         low, high = swap_halves(
             total[0:8, j * 128 : j * 128 + 128], total[8:16, j * 128 : j * 128 + 128]
         )
-        for half in range(2):
-            out_ref[half, 2 * j] = low
-            out_ref[half, 2 * j + 1] = high
+        low, high = low.astype(bf16), high.astype(bf16)
+        for copy in range(4):
+            out_ref[copy, 2 * j] = low
+            out_ref[copy, 2 * j + 1] = high
 
 
 def times_body(images_ref, table_ref, out_ref):
-    halves = []
-    for half in range(2):
-        total = images_ref[half, 0]
+    tm = lax.axis_index("tm")
+    blocks = []
+    for block in range(4):
+        total = images_ref[block, 0].astype(f32)
         for r in range(1, 8):
-            total = total + images_ref[half, r]
-        halves.append(total)
-    images = jnp.concatenate(halves, axis=0)
-    out_ref[...] = mm(block_of_table(table_ref), images, ((0,), (0,)))
+            total = total + images_ref[block, r].astype(f32)
+        blocks.append(total)
+    images = jnp.concatenate(blocks, axis=0)
+    table = table_ref[tm % 16 // 2, tm // 16 * 2 + tm % 2]
+    out_ref[...] = mm(table, images, ((0,), (0,)))
 
 
 def finish_body(sums_ref, data_ref, noise_ref, out_ref):
     total = sums_ref[0:8, :]
-    for r in range(1, 8):
+    for r in range(1, 4):
         total = total + sums_ref[r * 8 : r * 8 + 8, :]
     total = total[0:4, :] + total[4:8, :]
     noise = noise_ref[...]
@@ -231,6 +242,19 @@
         for block in range(16)
     ]
 
+    third = [
+        [
+            (half * 16 + z * 2 + core) * 8 + stripe
+            for half in range(2)
+            for core in range(2)
+            for stripe in range(8)
+        ]
+        for z in range(8)
+    ]
+    fourth = [
+        [half * 16 + z * 2 + core for z in range(8)] for half in range(2) for core in range(2)
+    ]
+
     spread = call(
         spread_body,
         jax.ShapeDtypeStruct((64, 128), f32),
@@ -258,20 +282,20 @@
     grids = exchange(grids, "stripe").reshape(128, 1024)
     images = call(
         images_body,
-        jax.ShapeDtypeStruct((2, 8, 8, 128), f32),
+        jax.ShapeDtypeStruct((4, 8, 8, 128), bf16),
         (grids, kernel, prior_spectrum.T, forward, backward, *columns),
         (whole(),) * 7,
         (pltpu.VMEM((128, 128), f32),),
         limit=20 << 20,
     )
-    images = exchange(images.reshape(16, 8, 128), ("tm", "stripe"), second)
+    images = exchange(images.reshape(32, 8, 128), ("tm", "stripe"), third)
     sums = call(
         times_body,
-        jax.ShapeDtypeStruct((64, 128), f32),
-        (images.reshape(2, 8, 8, 128), table),
+        jax.ShapeDtypeStruct((32, 128), f32),
+        (images.reshape(4, 8, 8, 128), jnp.asarray(inverse_table())),
         (whole(), whole()),
     )
-    sums = exchange(sums.reshape(16, 4, 128), "tm", first).reshape(64, 128)
+    sums = exchange(sums.reshape(8, 4, 128), "tm", fourth).reshape(32, 128)
     return call(
         finish_body,
         jax.ShapeDtypeStruct((4, 2, 64), f32),

time: 70.8 us -> 69.4 us (0.980)
  blocking collectives: 63.4 us -> 62.1 us
    all_to_all x5, blocking collectives: 63.4 us -> 62.1 us  [exchange(): return lax.all_to_all(x, axis, 0, 0, tiled=True, axis_index_groups=groups)]
where the time goes in v4:
time: 69.4 us; the launch traced here: 69.2 us
  blocking collectives  62.1 us (89%)
  Pallas kernels  6.2 us (9%)
  local copies, waits for them, and re-layouts  0.75 us (1%)
    all_to_all x5, blocking collectives, exchange(): return lax.all_to_all(x, axis, 0, 0, tiled=True, axis_index_groups=groups)  62.1 us
    pallas_call x6, Pallas kernels, call(): pl.pallas_call(body, out_shape=out_shape, in_specs=list(specs), out_specs...  6.2 us

profile of v4, /device:TPU:1, one launch (start us, length us, event | category | flops | bytes accessed | tf_op | source)
XLA Modules:
  0.0 69.2 jit_solution(9127495349482341230)
XLA Ops:
  0.0 0.0 copy-start.6
  0.0 0.7 copy-done.6
  0.7 0.0 copy-start.10
  0.7 0.1 shard_map.109
  0.8 17.4 %all_to_all.25 = f32[16,4,128]{2,1,0:T(4,128)S(1)} all-to-all(f32[16,4,128]{2,1,0:T(4,128)S(1)} %bitcast.22), channel_id=1, replica_groups={{0,8,16,24,32,40,48,56,64,72,80,88,96,104,112,120},{128,136,144,152,160..., dimensions={0} | all-to-all | bytes 65536 | tf_op jit(solution)/shard_map/all_to_all | solution.py:225
  18.2 0.0 copy-done.10
  18.2 0.0 copy-start.8
  18.2 0.2 shard_map.110
  18.4 0.0 copy-start.4
  18.4 0.0 copy-start.5
  18.4 13.3 %all_to_all.26 = f32[16,8,128]{2,1,0:T(8,128)S(1)} all-to-all(f32[16,8,128]{2,1,0:T(8,128)S(1)} %bitcast.18), channel_id=1, replica_groups={{0,1,2,3,4,5,6,7,128,129,130,131,132,133,134,135},{8,9,10,11,12,13,14,1..., dimensions={0} | all-to-all | bytes 131072 | tf_op jit(solution)/shard_map/all_to_all | solution.py:225
  31.7 0.0 slice-done
  31.7 0.0 slice-done.1
  31.7 0.0 copy-done.2
  31.7 0.0 copy-done.3
  31.7 0.0 copy-done.8
  31.8 0.0 copy-start
  31.8 0.0 copy-start.7
  31.8 0.0 copy-start.9
  31.8 2.1 %shard_map.111 = bf16[8,16,1024]{2,1,0:T(8,128)(2,1)S(1)} custom-call(f32[2,8,8,128]{3,2,1,0:T(8,128)S(1)} %bitcast.15, bf16[4,2,512,1024]{3,2,1,0:T(8,128)(2,1)S(1)} %bitcast.12, f32[4]{0:T(128)S(1)} %copy-done.8, bf16[128,128]{1,0:T(8,128)(2,1)S(1)} %copy-done.3, bf16[128,128]{1,0:T(8,128)(2,1)S(1)} %copy-done.2), custom_call_target="tpu_custom_call" | custom-call | flops 1000000 | bytes 100000 | tf_op jit(solution)/shard_map/pallas_call | solution.py:26
  33.9 8.6 %all_to_all.27 = bf16[8,16,1024]{2,1,0:T(8,128)(2,1)S(1)} all-to-all(bf16[8,16,1024]{2,1,0:T(8,128)(2,1)S(1)} %shard_map.111), channel_id=1, replica_groups=mesh['tm'=32,'stripe'=8] {'stripe'}, dimensions={0} | all-to-all | bytes 524288 | tf_op jit(solution)/shard_map/all_to_all | solution.py:225
  42.4 0.0 copy-done.1
  42.5 0.0 copy-done.4
  42.5 0.0 copy-done.5
  42.5 2.9 %shard_map.112 = bf16[4,8,8,128]{3,2,1,0:T(8,128)(2,1)S(1)} custom-call(bf16[128,1024]{1,0:T(8,128)(2,1)S(1)} %bitcast.13, bf16[4,2,512,1024]{3,2,1,0:T(8,128)(2,1)S(1)} %bitcast.12, f32[64,128]{1,0:T(8,128)S(1)} %bitcast.20, bf16[128,256]{1,0:T(8,128)(2,1)S(1)} %copy-done.4, bf16[8,32,256]{2,1,0:T(8,128)(2,1)S(1)} %copy-done.1, ...), custom_call_target="tpu_custom_call" | custom-call | flops 1000000 | bytes 100000 | tf_op jit(solution)/shard_map/pallas_call | solution.py:26
  45.4 13.8 %all_to_all.28 = bf16[32,8,128]{2,1,0:T(8,128)(2,1)S(1)} all-to-all(bf16[32,8,128]{2,1,0:T(8,128)(2,1)S(1)} %bitcast.14), channel_id=1, replica_groups={{0,1,2,3,4,5,6,7,8,9,10,11,12,13,14,15,128,129,130,131,132,133,134,135,..., dimensions={0} | all-to-all | bytes 131072 | tf_op jit(solution)/shard_map/all_to_all | solution.py:225
  59.2 0.0 copy-done
  59.2 0.2 shard_map.113
  59.4 9.0 %all_to_all.29 = f32[8,4,128]{2,1,0:T(4,128)S(1)} all-to-all(f32[8,4,128]{2,1,0:T(4,128)S(1)} %bitcast.17), channel_id=1, replica_groups={{0,16,32,48,64,80,96,112},{8,24,40,56,72,88,104,120},{128,144,160,176,1..., dimensions={0} | all-to-all | bytes 32768 | tf_op jit(solution)/shard_map/all_to_all | solution.py:225
  68.4 0.0 copy-done.7
  68.4 0.0 copy-done.9
  68.4 0.7 %shard_map.114 = f32[4,2,64]{2,1,0:T(2,128)} custom-call(f32[32,128]{1,0:T(8,128)S(1)} %bitcast.19, f32[4,2,64]{2,1,0:T(2,128)S(1)} %copy-done.7, f32[1,64]{1,0:T(1,128)S(1)} %bitcast.23), custom_call_target="tpu_custom_call" | custom-call | flops 1000000 | bytes 100000 | tf_op jit(solution)/shard_map/pallas_call | solution.py:26
  (6 shorter events, 0.0 us)
Async XLA Ops:
  0.0 0.7 copy-start.6
  0.7 17.5 %copy-start.10 = (f32[2,16,16,64]{3,2,1,0:T(8,128)S(1)}, f32[2,16,16,64]{3,2,1,0:T(8,128)}, u32[]{:S(2)}) copy-start(f32[2,16,16,64]{3,2,1,0:T(8,128)} %constant.12.clone.table_ref) | copy-start | bytes 393220
  0.7 31.0 %slice-start = ((s8[8388608]{0:T(1024)(128)(4,1)}), s8[4194304]{0:T(1024)(128)(4,1)S(1)}, s32[]{:S(2)}) async-start(s8[8388608]{0:T(1024)(128)(4,1)} %bitcast.11), calls=%async_computation.5 | async-start | bytes 8388608
  18.2 13.5 %slice-start.1 = ((s8[8388608]{0:T(1024)(128)(4,1)}), s8[4194304]{0:T(1024)(128)(4,1)S(1)}, s32[]{:S(2)}) async-start(s8[8388608]{0:T(1024)(128)(4,1)} %bitcast.11), calls=%async_computation.6 | async-start | bytes 8388608
  18.2 13.5 %copy-start.2 = (bf16[128,128]{1,0:T(8,128)(2,1)S(1)}, bf16[128,128]{1,0:T(8,128)(2,1)}, u32[]{:S(2)}) copy-start(bf16[128,128]{1,0:T(8,128)(2,1)} %constant.16.clone.low_ref) | copy-start | bytes 98308
  18.2 13.6 %copy-start.3 = (bf16[128,128]{1,0:T(8,128)(2,1)S(1)}, bf16[128,128]{1,0:T(8,128)(2,1)}, u32[]{:S(2)}) copy-start(bf16[128,128]{1,0:T(8,128)(2,1)} %constant.15.clone.high_ref) | copy-start | bytes 98308
  18.2 13.6 %copy-start.8 = (f32[4]{0:T(128)S(1)}, f32[4]{0:T(128)}, u32[]{:S(2)}) copy-start(f32[4]{0:T(128)} %scale_ref.1) | copy-start | bytes 52
  18.4 24.1 %copy-start.1 = (bf16[8,32,256]{2,1,0:T(8,128)(2,1)S(1)}, bf16[8,32,256]{2,1,0:T(8,128)(2,1)}, u32[]{:S(2)}) copy-start(bf16[8,32,256]{2,1,0:T(8,128)(2,1)} %constant.14.clone.backward_ref) | copy-start | bytes 393220
  18.4 24.1 %copy-start.4 = (bf16[128,256]{1,0:T(8,128)(2,1)S(1)}, bf16[128,256]{1,0:T(8,128)(2,1)}, u32[]{:S(2)}) copy-start(bf16[128,256]{1,0:T(8,128)(2,1)} %constant.13.clone.forward_ref) | copy-start | bytes 196612
  18.4 24.1 %copy-start.5 = (f32[128,64]{0,1:T(8,128)S(1)}, f32[128,64]{0,1:T(8,128)}, u32[]{:S(2)}) copy-start(f32[128,64]{0,1:T(8,128)} %param.14) | copy-start | bytes 98308
  31.8 27.4 %copy-start = (f32[8,4,32,32]{3,2,1,0:T(8,128)S(1)}, f32[8,4,32,32]{3,2,1,0:T(8,128)}, u32[]{:S(2)}) copy-start(f32[8,4,32,32]{3,2,1,0:T(8,128)} %constant.17.clone.table_ref) | copy-start | bytes 393220
  31.8 36.6 %copy-start.7 = (f32[4,2,64]{2,1,0:T(2,128)S(1)}, f32[4,2,64]{2,1,0:T(2,128)}, u32[]{:S(2)}) copy-start(f32[4,2,64]{2,1,0:T(2,128)} %data_ref.3) | copy-start | bytes 6148
  31.8 36.6 %copy-start.9 = (f32[64]{0:T(128)S(1)}, f32[64]{0:T(128)}, u32[]{:S(2)}) copy-start(f32[64]{0:T(128)} %param.15) | copy-start | bytes 772

commit v5 on v4

--- a/solution.py
+++ b/solution.py
@@ -1,4 +1,3 @@
-import functools
 import math
 
 import jax
@@ -7,6 +6,7 @@
 from jax import lax
 from jax.experimental import pallas as pl
 from jax.experimental.pallas import tpu as pltpu
+from jax.sharding import Mesh
 from jax.sharding import PartitionSpec as P
 
 exact = lax.Precision.HIGHEST
@@ -108,8 +108,7 @@
 
 
 def block_of_table(table_ref):
-    tm = lax.axis_index("tm")
-    return table_ref[tm // 16, tm % 16]
+    return table_ref[lax.axis_index("x_hi"), lax.axis_index("z") * 2 + lax.axis_index("core")]
 
 
 def spectra_body(data_ref, table_ref, out_ref):
@@ -199,7 +198,7 @@
 
 
 def times_body(images_ref, table_ref, out_ref):
-    tm = lax.axis_index("tm")
+    half = lax.axis_index("x_hi") * 2 + lax.axis_index("core")
     blocks = []
     for block in range(4):
         total = images_ref[block, 0].astype(f32)
@@ -207,7 +206,7 @@
             total = total + images_ref[block, r].astype(f32)
         blocks.append(total)
     images = jnp.concatenate(blocks, axis=0)
-    table = table_ref[tm % 16 // 2, tm // 16 * 2 + tm % 2]
+    table = table_ref[lax.axis_index("z"), half]
     out_ref[...] = mm(table, images, ((0,), (0,)))
 
 
@@ -221,8 +220,8 @@
     out_ref[:, 1, :] = total[:, 64:128] + noise * data_ref[:, 1, :]
 
 
-def exchange(x, axis, groups=None):
-    return lax.all_to_all(x, axis, 0, 0, tiled=True, axis_index_groups=groups)
+def exchange(x, axes):
+    return lax.all_to_all(x, axes, 0, 0, tiled=True)
 
 
 def shards(data_vec, kernel, time_spectrum, prior_spectrum, noise_var):
@@ -236,25 +235,6 @@
     backward = jnp.asarray(np.concatenate([upper, lower], axis=1))
     columns = [jnp.asarray(t) for t in split_table(np.kron(np.eye(2), sine_matrix(64)))]
 
-    first = [[half * 16 + block for block in range(16)] for half in range(2)]
-    second = [
-        [(half * 16 + block) * 8 + stripe for half in range(2) for stripe in range(8)]
-        for block in range(16)
-    ]
-
-    third = [
-        [
-            (half * 16 + z * 2 + core) * 8 + stripe
-            for half in range(2)
-            for core in range(2)
-            for stripe in range(8)
-        ]
-        for z in range(8)
-    ]
-    fourth = [
-        [half * 16 + z * 2 + core for z in range(8)] for half in range(2) for core in range(2)
-    ]
-
     spread = call(
         spread_body,
         jax.ShapeDtypeStruct((64, 128), f32),
@@ -262,7 +242,7 @@
         (whole(),),
         hint=2e10,
     )
-    by_time = exchange(spread.reshape(16, 4, 128), "tm", first).reshape(64, 128)
+    by_time = exchange(spread.reshape(16, 4, 128), ("z", "core")).reshape(64, 128)
     spectra = call(
         spectra_body,
         jax.ShapeDtypeStruct((2, 8, 8, 128), f32),
@@ -270,7 +250,7 @@
         (whole(), whole()),
         hint=2e10,
     )
-    gathered = exchange(spectra.reshape(16, 8, 128), ("tm", "stripe"), second)
+    gathered = exchange(spectra.reshape(16, 8, 128), ("x_hi", "stripe"))
     grids = call(
         adjoint_body,
         jax.ShapeDtypeStruct((8, 16, 1024), bf16),
@@ -288,14 +268,14 @@
         (pltpu.VMEM((128, 128), f32),),
         limit=20 << 20,
     )
-    images = exchange(images.reshape(32, 8, 128), ("tm", "stripe"), third)
+    images = exchange(images.reshape(32, 8, 128), ("x_hi", "core", "stripe"))
     sums = call(
         times_body,
         jax.ShapeDtypeStruct((32, 128), f32),
         (images.reshape(4, 8, 8, 128), jnp.asarray(inverse_table())),
         (whole(), whole()),
     )
-    sums = exchange(sums.reshape(8, 4, 128), "tm", fourth).reshape(32, 128)
+    sums = exchange(sums.reshape(8, 4, 128), "z").reshape(32, 128)
     return call(
         finish_body,
         jax.ShapeDtypeStruct((4, 2, 64), f32),
@@ -305,16 +285,18 @@
 
 
 def solution(mesh):
+    fine = Mesh(mesh.devices.reshape(2, 8, 2, 8), ("x_hi", "z", "core", "stripe"))
+    tm = ("x_hi", "z", "core")
     return jax.shard_map(
         shards,
-        mesh=mesh,
+        mesh=fine,
         in_specs=(
-            P("tm", None, "stripe"),
-            P("tm", None, None, "stripe"),
-            P("tm"),
+            P(tm, None, "stripe"),
+            P(tm, None, None, "stripe"),
+            P(tm),
             P(),
             P("stripe"),
         ),
-        out_specs=P("tm", None, "stripe"),
+        out_specs=P(tm, None, "stripe"),
         check_vma=False,
     )

time: 69.4 us -> 69.4 us (level)
  no operation moved by 1% of the time
where the time goes in v5:
time: 69.4 us; the launch traced here: 69.2 us
  blocking collectives  62.1 us (89%)
  Pallas kernels  6.19 us (9%)
  local copies, waits for them, and re-layouts  0.75 us (1%)
    all_to_all x5, blocking collectives, exchange(): return lax.all_to_all(x, axes, 0, 0, tiled=True)  62.1 us
    pallas_call x6, Pallas kernels, call(): pl.pallas_call(body, out_shape=out_shape, in_specs=list(specs), out_specs...  6.19 us

profile of v5, /device:TPU:1, one launch (start us, length us, event | category | flops | bytes accessed | tf_op | source)
XLA Modules:
  0.0 69.2 jit_solution(17570976054567198917)
XLA Ops:
  0.0 0.0 copy-start.6
  0.0 0.7 copy-done.6
  0.7 0.0 copy-start.10
  0.7 0.1 shard_map.109
  0.8 17.4 %all_to_all.25 = f32[16,4,128]{2,1,0:T(4,128)S(1)} all-to-all(f32[16,4,128]{2,1,0:T(4,128)S(1)} %bitcast.22), channel_id=1, replica_groups=mesh['x_hi'=2,'z'=8,'core'=2,'stripe'=8] {'z','core'}, dimensions={0} | all-to-all | bytes 65536 | tf_op jit(solution)/shard_map/all_to_all | solution.py:224
  18.2 0.0 copy-done.10
  18.2 0.0 copy-start.8
  18.2 0.2 shard_map.110
  18.4 0.0 copy-start.4
  18.4 0.0 copy-start.5
  18.4 13.3 %all_to_all.26 = f32[16,8,128]{2,1,0:T(8,128)S(1)} all-to-all(f32[16,8,128]{2,1,0:T(8,128)S(1)} %bitcast.18), channel_id=1, replica_groups=mesh['x_hi'=2,'z'=8,'core'=2,'stripe'=8] {'x_hi','stripe'}, dimensions={0} | all-to-all | bytes 131072 | tf_op jit(solution)/shard_map/all_to_all | solution.py:224
  31.7 0.0 slice-done
  31.7 0.0 slice-done.1
  31.7 0.0 copy-done.2
  31.7 0.0 copy-done.3
  31.7 0.0 copy-done.8
  31.8 0.0 copy-start
  31.8 0.0 copy-start.7
  31.8 0.0 copy-start.9
  31.8 2.1 %shard_map.111 = bf16[8,16,1024]{2,1,0:T(8,128)(2,1)S(1)} custom-call(f32[2,8,8,128]{3,2,1,0:T(8,128)S(1)} %bitcast.15, bf16[4,2,512,1024]{3,2,1,0:T(8,128)(2,1)S(1)} %bitcast.12, f32[4]{0:T(128)S(1)} %copy-done.8, bf16[128,128]{1,0:T(8,128)(2,1)S(1)} %copy-done.3, bf16[128,128]{1,0:T(8,128)(2,1)S(1)} %copy-done.2), custom_call_target="tpu_custom_call" | custom-call | flops 1000000 | bytes 100000 | tf_op jit(solution)/shard_map/pallas_call | solution.py:26
  33.9 8.6 %all_to_all.27 = bf16[8,16,1024]{2,1,0:T(8,128)(2,1)S(1)} all-to-all(bf16[8,16,1024]{2,1,0:T(8,128)(2,1)S(1)} %shard_map.111), channel_id=1, replica_groups=mesh['x_hi'=2,'z'=8,'core'=2,'stripe'=8] {'stripe'}, dimensions={0} | all-to-all | bytes 524288 | tf_op jit(solution)/shard_map/all_to_all | solution.py:224
  42.4 0.0 copy-done.1
  42.4 0.0 copy-done.4
  42.5 0.0 copy-done.5
  42.5 2.9 %shard_map.112 = bf16[4,8,8,128]{3,2,1,0:T(8,128)(2,1)S(1)} custom-call(bf16[128,1024]{1,0:T(8,128)(2,1)S(1)} %bitcast.13, bf16[4,2,512,1024]{3,2,1,0:T(8,128)(2,1)S(1)} %bitcast.12, f32[64,128]{1,0:T(8,128)S(1)} %bitcast.20, bf16[128,256]{1,0:T(8,128)(2,1)S(1)} %copy-done.4, bf16[8,32,256]{2,1,0:T(8,128)(2,1)S(1)} %copy-done.1, ...), custom_call_target="tpu_custom_call" | custom-call | flops 1000000 | bytes 100000 | tf_op jit(solution)/shard_map/pallas_call | solution.py:26
  45.4 13.8 %all_to_all.28 = bf16[32,8,128]{2,1,0:T(8,128)(2,1)S(1)} all-to-all(bf16[32,8,128]{2,1,0:T(8,128)(2,1)S(1)} %bitcast.14), channel_id=1, replica_groups=mesh['x_hi'=2,'z'=8,'core'=2,'stripe'=8] {'x_hi','core','stripe'}, dimensions={0} | all-to-all | bytes 131072 | tf_op jit(solution)/shard_map/all_to_all | solution.py:224
  59.2 0.0 copy-done
  59.2 0.2 shard_map.113
  59.4 9.0 %all_to_all.29 = f32[8,4,128]{2,1,0:T(4,128)S(1)} all-to-all(f32[8,4,128]{2,1,0:T(4,128)S(1)} %bitcast.17), channel_id=1, replica_groups=mesh['x_hi'=2,'z'=8,'core'=2,'stripe'=8] {'z'}, dimensions={0} | all-to-all | bytes 32768 | tf_op jit(solution)/shard_map/all_to_all | solution.py:224
  68.4 0.0 copy-done.7
  68.4 0.0 copy-done.9
  68.4 0.7 %shard_map.114 = f32[4,2,64]{2,1,0:T(2,128)} custom-call(f32[32,128]{1,0:T(8,128)S(1)} %bitcast.19, f32[4,2,64]{2,1,0:T(2,128)S(1)} %copy-done.7, f32[1,64]{1,0:T(1,128)S(1)} %bitcast.23), custom_call_target="tpu_custom_call" | custom-call | flops 1000000 | bytes 100000 | tf_op jit(solution)/shard_map/pallas_call | solution.py:26
  (6 shorter events, 0.0 us)
Async XLA Ops:
  0.0 0.7 copy-start.6
  0.7 17.5 %copy-start.10 = (f32[2,16,16,64]{3,2,1,0:T(8,128)S(1)}, f32[2,16,16,64]{3,2,1,0:T(8,128)}, u32[]{:S(2)}) copy-start(f32[2,16,16,64]{3,2,1,0:T(8,128)} %constant.12.clone.table_ref) | copy-start | bytes 393220
  0.7 31.0 %slice-start = ((s8[8388608]{0:T(1024)(128)(4,1)}), s8[4194304]{0:T(1024)(128)(4,1)S(1)}, s32[]{:S(2)}) async-start(s8[8388608]{0:T(1024)(128)(4,1)} %bitcast.11), calls=%async_computation.5 | async-start | bytes 8388608
  18.2 13.5 %slice-start.1 = ((s8[8388608]{0:T(1024)(128)(4,1)}), s8[4194304]{0:T(1024)(128)(4,1)S(1)}, s32[]{:S(2)}) async-start(s8[8388608]{0:T(1024)(128)(4,1)} %bitcast.11), calls=%async_computation.6 | async-start | bytes 8388608
  18.2 13.5 %copy-start.2 = (bf16[128,128]{1,0:T(8,128)(2,1)S(1)}, bf16[128,128]{1,0:T(8,128)(2,1)}, u32[]{:S(2)}) copy-start(bf16[128,128]{1,0:T(8,128)(2,1)} %constant.16.clone.low_ref) | copy-start | bytes 98308
  18.2 13.5 %copy-start.3 = (bf16[128,128]{1,0:T(8,128)(2,1)S(1)}, bf16[128,128]{1,0:T(8,128)(2,1)}, u32[]{:S(2)}) copy-start(bf16[128,128]{1,0:T(8,128)(2,1)} %constant.15.clone.high_ref) | copy-start | bytes 98308
  18.2 13.6 %copy-start.8 = (f32[4]{0:T(128)S(1)}, f32[4]{0:T(128)}, u32[]{:S(2)}) copy-start(f32[4]{0:T(128)} %scale_ref.1) | copy-start | bytes 52
  18.4 24.1 %copy-start.1 = (bf16[8,32,256]{2,1,0:T(8,128)(2,1)S(1)}, bf16[8,32,256]{2,1,0:T(8,128)(2,1)}, u32[]{:S(2)}) copy-start(bf16[8,32,256]{2,1,0:T(8,128)(2,1)} %constant.14.clone.backward_ref) | copy-start | bytes 393220
  18.4 24.1 %copy-start.4 = (bf16[128,256]{1,0:T(8,128)(2,1)S(1)}, bf16[128,256]{1,0:T(8,128)(2,1)}, u32[]{:S(2)}) copy-start(bf16[128,256]{1,0:T(8,128)(2,1)} %constant.13.clone.forward_ref) | copy-start | bytes 196612
  18.4 24.1 %copy-start.5 = (f32[128,64]{0,1:T(8,128)S(1)}, f32[128,64]{0,1:T(8,128)}, u32[]{:S(2)}) copy-start(f32[128,64]{0,1:T(8,128)} %param.14) | copy-start | bytes 98308
  31.8 27.4 %copy-start = (f32[8,4,32,32]{3,2,1,0:T(8,128)S(1)}, f32[8,4,32,32]{3,2,1,0:T(8,128)}, u32[]{:S(2)}) copy-start(f32[8,4,32,32]{3,2,1,0:T(8,128)} %constant.17.clone.table_ref) | copy-start | bytes 393220
  31.8 36.6 %copy-start.7 = (f32[4,2,64]{2,1,0:T(2,128)S(1)}, f32[4,2,64]{2,1,0:T(2,128)}, u32[]{:S(2)}) copy-start(f32[4,2,64]{2,1,0:T(2,128)} %data_ref.3) | copy-start | bytes 6148
  31.8 36.6 %copy-start.9 = (f32[64]{0:T(128)S(1)}, f32[64]{0:T(128)}, u32[]{:S(2)}) copy-start(f32[64]{0:T(128)} %param.15) | copy-start | bytes 772

commit v6 on v5

--- a/solution.py
+++ b/solution.py
@@ -93,11 +93,8 @@
 
 def column_transform(x, high_ref, low_ref):
     high, low = split(x)
-    return (
-        mm(high, high_ref[...], precision=None)
-        + mm(low, high_ref[...], precision=None)
-        + mm(high, low_ref[...], precision=None)
-    )
+    both = mm(jnp.concatenate([high, low], axis=0), high_ref[...], precision=None)
+    return both[:128] + both[128:] + mm(high, low_ref[...], precision=None)
 
 
 def spread_body(data_ref, out_ref):
@@ -176,11 +173,15 @@
     smooth = column_transform(grid_ref[...], high_ref, low_ref)
     smooth = jnp.concatenate([smooth[c * 16 : c * 16 + 16, :] for c in range(8)], axis=1)
     left = smooth.astype(bf16)
-    products = mm(left, kernel_ref[...].reshape(4096, 1024), ((1,), (1,)), precision=None)
     freq = lax.broadcasted_iota(jnp.int32, (16, 1024), 0) % 4
-    total = jnp.where(freq == 0, products[:, 0:1024], 0.0)
-    for k in range(1, 4):
-        total = jnp.where(freq == k, products[:, k * 1024 : k * 1024 + 1024], total)
+    total = None
+    for k in range(4):
+        term = None
+        for c in range(4):
+            right = kernel_ref[k, :, :, c * 256 : c * 256 + 256].reshape(1024, 256)
+            piece = mm(left[:, c * 256 : c * 256 + 256], right, ((1,), (1,)), precision=None)
+            term = piece if term is None else term + piece
+        total = term if k == 0 else jnp.where(freq == k, term, total)
     sub = lax.broadcasted_iota(jnp.int32, (8, 512), 0)
     rows = []
     for n in range(2):

time: 69.4 us -> 69.4 us (level)
  no operation moved by 1% of the time
where the time goes in v6:
time: 69.4 us; the launch traced here: 69.1 us
  blocking collectives  62.1 us (89%)
  Pallas kernels  6.17 us (9%)
  local copies, waits for them, and re-layouts  0.75 us (1%)
    all_to_all x5, blocking collectives, exchange(): return lax.all_to_all(x, axes, 0, 0, tiled=True)  62.1 us
    pallas_call x6, Pallas kernels, call(): pl.pallas_call(body, out_shape=out_shape, in_specs=list(specs), out_specs...  6.17 us

profile of v6, /device:TPU:1, one launch (start us, length us, event | category | flops | bytes accessed | tf_op | source)
XLA Modules:
  0.0 69.1 jit_solution(5777034073821100775)
XLA Ops:
  0.0 0.0 copy-start.6
  0.0 0.7 copy-done.6
  0.7 0.0 copy-start.10
  0.7 0.1 shard_map.109
  0.8 17.4 %all_to_all.25 = f32[16,4,128]{2,1,0:T(4,128)S(1)} all-to-all(f32[16,4,128]{2,1,0:T(4,128)S(1)} %bitcast.22), channel_id=1, replica_groups=mesh['x_hi'=2,'z'=8,'core'=2,'stripe'=8] {'z','core'}, dimensions={0} | all-to-all | bytes 65536 | tf_op jit(solution)/shard_map/all_to_all | solution.py:225
  18.2 0.0 copy-done.10
  18.2 0.0 copy-start.8
  18.2 0.2 shard_map.110
  18.4 0.0 copy-start.4
  18.4 0.0 copy-start.5
  18.4 13.3 %all_to_all.26 = f32[16,8,128]{2,1,0:T(8,128)S(1)} all-to-all(f32[16,8,128]{2,1,0:T(8,128)S(1)} %bitcast.18), channel_id=1, replica_groups=mesh['x_hi'=2,'z'=8,'core'=2,'stripe'=8] {'x_hi','stripe'}, dimensions={0} | all-to-all | bytes 131072 | tf_op jit(solution)/shard_map/all_to_all | solution.py:225
  31.7 0.0 slice-done
  31.7 0.0 slice-done.1
  31.7 0.0 copy-done.2
  31.7 0.0 copy-done.3
  31.7 0.0 copy-done.8
  31.8 0.0 copy-start
  31.8 0.0 copy-start.7
  31.8 0.0 copy-start.9
  31.8 2.1 %shard_map.111 = bf16[8,16,1024]{2,1,0:T(8,128)(2,1)S(1)} custom-call(f32[2,8,8,128]{3,2,1,0:T(8,128)S(1)} %bitcast.15, bf16[4,2,512,1024]{3,2,1,0:T(8,128)(2,1)S(1)} %bitcast.12, f32[4]{0:T(128)S(1)} %copy-done.8, bf16[128,128]{1,0:T(8,128)(2,1)S(1)} %copy-done.3, bf16[128,128]{1,0:T(8,128)(2,1)S(1)} %copy-done.2), custom_call_target="tpu_custom_call" | custom-call | flops 1000000 | bytes 100000 | tf_op jit(solution)/shard_map/pallas_call | solution.py:26
  33.9 8.6 %all_to_all.27 = bf16[8,16,1024]{2,1,0:T(8,128)(2,1)S(1)} all-to-all(bf16[8,16,1024]{2,1,0:T(8,128)(2,1)S(1)} %shard_map.111), channel_id=1, replica_groups=mesh['x_hi'=2,'z'=8,'core'=2,'stripe'=8] {'stripe'}, dimensions={0} | all-to-all | bytes 524288 | tf_op jit(solution)/shard_map/all_to_all | solution.py:225
  42.4 0.0 copy-done.1
  42.4 0.0 copy-done.4
  42.4 0.0 copy-done.5
  42.5 2.9 %shard_map.112 = bf16[4,8,8,128]{3,2,1,0:T(8,128)(2,1)S(1)} custom-call(bf16[128,1024]{1,0:T(8,128)(2,1)S(1)} %bitcast.13, bf16[4,2,512,1024]{3,2,1,0:T(8,128)(2,1)S(1)} %bitcast.12, f32[64,128]{1,0:T(8,128)S(1)} %bitcast.20, bf16[128,256]{1,0:T(8,128)(2,1)S(1)} %copy-done.4, bf16[8,32,256]{2,1,0:T(8,128)(2,1)S(1)} %copy-done.1, ...), custom_call_target="tpu_custom_call" | custom-call | flops 1000000 | bytes 100000 | tf_op jit(solution)/shard_map/pallas_call | solution.py:26
  45.4 13.8 %all_to_all.28 = bf16[32,8,128]{2,1,0:T(8,128)(2,1)S(1)} all-to-all(bf16[32,8,128]{2,1,0:T(8,128)(2,1)S(1)} %bitcast.14), channel_id=1, replica_groups=mesh['x_hi'=2,'z'=8,'core'=2,'stripe'=8] {'x_hi','core','stripe'}, dimensions={0} | all-to-all | bytes 131072 | tf_op jit(solution)/shard_map/all_to_all | solution.py:225
  59.2 0.0 copy-done
  59.2 0.2 shard_map.113
  59.4 9.0 %all_to_all.29 = f32[8,4,128]{2,1,0:T(4,128)S(1)} all-to-all(f32[8,4,128]{2,1,0:T(4,128)S(1)} %bitcast.17), channel_id=1, replica_groups=mesh['x_hi'=2,'z'=8,'core'=2,'stripe'=8] {'z'}, dimensions={0} | all-to-all | bytes 32768 | tf_op jit(solution)/shard_map/all_to_all | solution.py:225
  68.4 0.0 copy-done.7
  68.4 0.0 copy-done.9
  68.4 0.7 %shard_map.114 = f32[4,2,64]{2,1,0:T(2,128)} custom-call(f32[32,128]{1,0:T(8,128)S(1)} %bitcast.19, f32[4,2,64]{2,1,0:T(2,128)S(1)} %copy-done.7, f32[1,64]{1,0:T(1,128)S(1)} %bitcast.23), custom_call_target="tpu_custom_call" | custom-call | flops 1000000 | bytes 100000 | tf_op jit(solution)/shard_map/pallas_call | solution.py:26
  (6 shorter events, 0.0 us)
Async XLA Ops:
  0.0 0.7 copy-start.6
  0.7 17.5 %copy-start.10 = (f32[2,16,16,64]{3,2,1,0:T(8,128)S(1)}, f32[2,16,16,64]{3,2,1,0:T(8,128)}, u32[]{:S(2)}) copy-start(f32[2,16,16,64]{3,2,1,0:T(8,128)} %constant.12.clone.table_ref) | copy-start | bytes 393220
  0.7 31.0 %slice-start = ((s8[8388608]{0:T(1024)(128)(4,1)}), s8[4194304]{0:T(1024)(128)(4,1)S(1)}, s32[]{:S(2)}) async-start(s8[8388608]{0:T(1024)(128)(4,1)} %bitcast.11), calls=%async_computation.5 | async-start | bytes 8388608
  18.2 13.5 %slice-start.1 = ((s8[8388608]{0:T(1024)(128)(4,1)}), s8[4194304]{0:T(1024)(128)(4,1)S(1)}, s32[]{:S(2)}) async-start(s8[8388608]{0:T(1024)(128)(4,1)} %bitcast.11), calls=%async_computation.6 | async-start | bytes 8388608
  18.2 13.5 %copy-start.2 = (bf16[128,128]{1,0:T(8,128)(2,1)S(1)}, bf16[128,128]{1,0:T(8,128)(2,1)}, u32[]{:S(2)}) copy-start(bf16[128,128]{1,0:T(8,128)(2,1)} %constant.16.clone.low_ref) | copy-start | bytes 98308
  18.2 13.5 %copy-start.3 = (bf16[128,128]{1,0:T(8,128)(2,1)S(1)}, bf16[128,128]{1,0:T(8,128)(2,1)}, u32[]{:S(2)}) copy-start(bf16[128,128]{1,0:T(8,128)(2,1)} %constant.15.clone.high_ref) | copy-start | bytes 98308
  18.2 13.6 %copy-start.8 = (f32[4]{0:T(128)S(1)}, f32[4]{0:T(128)}, u32[]{:S(2)}) copy-start(f32[4]{0:T(128)} %scale_ref.1) | copy-start | bytes 52
  18.4 24.1 %copy-start.1 = (bf16[8,32,256]{2,1,0:T(8,128)(2,1)S(1)}, bf16[8,32,256]{2,1,0:T(8,128)(2,1)}, u32[]{:S(2)}) copy-start(bf16[8,32,256]{2,1,0:T(8,128)(2,1)} %constant.14.clone.backward_ref) | copy-start | bytes 393220
  18.4 24.1 %copy-start.4 = (bf16[128,256]{1,0:T(8,128)(2,1)S(1)}, bf16[128,256]{1,0:T(8,128)(2,1)}, u32[]{:S(2)}) copy-start(bf16[128,256]{1,0:T(8,128)(2,1)} %constant.13.clone.forward_ref) | copy-start | bytes 196612
  18.4 24.1 %copy-start.5 = (f32[128,64]{0,1:T(8,128)S(1)}, f32[128,64]{0,1:T(8,128)}, u32[]{:S(2)}) copy-start(f32[128,64]{0,1:T(8,128)} %param.14) | copy-start | bytes 98308
  31.8 27.4 %copy-start = (f32[8,4,32,32]{3,2,1,0:T(8,128)S(1)}, f32[8,4,32,32]{3,2,1,0:T(8,128)}, u32[]{:S(2)}) copy-start(f32[8,4,32,32]{3,2,1,0:T(8,128)} %constant.17.clone.table_ref) | copy-start | bytes 393220
  31.8 36.6 %copy-start.7 = (f32[4,2,64]{2,1,0:T(2,128)S(1)}, f32[4,2,64]{2,1,0:T(2,128)}, u32[]{:S(2)}) copy-start(f32[4,2,64]{2,1,0:T(2,128)} %data_ref.3) | copy-start | bytes 6148
  31.8 36.6 %copy-start.9 = (f32[64]{0:T(128)S(1)}, f32[64]{0:T(128)}, u32[]{:S(2)}) copy-start(f32[64]{0:T(128)} %param.15) | copy-start | bytes 772

commit v7 on v6

--- a/solution.py
+++ b/solution.py
@@ -9,17 +9,12 @@
 from jax.sharding import Mesh
 from jax.sharding import PartitionSpec as P
 
-exact = lax.Precision.HIGHEST
 f32 = jnp.float32
 bf16 = jnp.bfloat16
 
 
 def whole():
     return pl.BlockSpec(memory_space=pltpu.VMEM)
-
-
-def scalars():
-    return pl.BlockSpec(memory_space=pltpu.SMEM)
 
 
 def call(body, out_shape, operands, specs, scratch=(), limit=4 << 20, hint=1e6):
@@ -36,9 +31,9 @@
     )(*operands)
 
 
-def mm(a, b, dims=((1,), (0,)), precision=exact):
+def mm(a, b, dims=((1,), (0,))):
     return lax.dot_general(
-        a, b, (dims, ((), ())), precision=precision, preferred_element_type=f32
+        a, b, (dims, ((), ())), preferred_element_type=f32
     )
 
 
@@ -47,7 +42,7 @@
     angles = np.outer(steps, steps) % 256 * (math.pi / 128)
     pair = np.stack([np.cos(angles), -np.sin(angles)]) / math.sqrt(128)
     pair = pair.reshape(2, halves, blocks, 4, halves, 64).transpose(4, 2, 1, 0, 3, 5)
-    return pair.reshape(halves, blocks, halves * 8, 64).astype(np.float32)
+    return triple_table(pair.reshape(halves, blocks, halves * 8, 64))
 
 
 def inverse_table():
@@ -55,8 +50,8 @@
     angles = np.outer(steps, steps) % 256 * (math.pi / 128)
     pair = np.stack([np.cos(angles), -np.sin(angles)]) / math.sqrt(128)
     pair = pair.reshape(2, 2, 8, 2, 4, 2, 8, 2, 4)
-    pair = pair.transpose(2, 5, 7, 1, 3, 0, 4, 6, 8)
-    return pair.reshape(8, 4, 32, 32).astype(np.float32)
+    pair = pair.transpose(2, 5, 7, 6, 8, 1, 3, 0, 4)
+    return triple_table(pair.reshape(8, 4, 32, 32))
 
 
 def sine_matrix(length):
@@ -91,10 +86,20 @@
     return high, (x - high.astype(np.float64)).astype(np.float32).astype(bf16)
 
 
+def triple_table(x):
+    high, low = split_table(x)
+    return np.concatenate([high, high, low], axis=-1)
+
+
+def triple_product(table, x):
+    high, low = split(x)
+    return mm(table, jnp.concatenate([high, low, high], axis=0))
+
+
 def column_transform(x, high_ref, low_ref):
     high, low = split(x)
-    both = mm(jnp.concatenate([high, low], axis=0), high_ref[...], precision=None)
-    return both[:128] + both[128:] + mm(high, low_ref[...], precision=None)
+    both = mm(jnp.concatenate([high, low], axis=0), high_ref[...])
+    return both[:128] + both[128:] + mm(high, low_ref[...])
 
 
 def spread_body(data_ref, out_ref):
@@ -109,7 +114,7 @@
 
 
 def spectra_body(data_ref, table_ref, out_ref):
-    spectra = mm(block_of_table(table_ref), data_ref[...])
+    spectra = triple_product(block_of_table(table_ref), data_ref[...])
     for half in range(2):
         for r in range(8):
             out_ref[half, r] = spectra[half * 8 : half * 8 + 8, :]
@@ -133,14 +138,13 @@
     total = None
     for k in range(4):
         left = jnp.where(freq == k, both, 0.0).astype(bf16)
-        term = mm(left, kernel_ref[k].reshape(1024, 1024), precision=None)
+        term = mm(left, kernel_ref[k].reshape(1024, 1024))
         total = term if total is None else total + term
-    row = lax.broadcasted_iota(jnp.int32, (16, 1024), 0) % 4
-    scale = jnp.where(
-        row < 2,
-        jnp.where(row == 0, scale_ref[0], scale_ref[1]),
-        jnp.where(row == 2, scale_ref[2], scale_ref[3]),
-    )
+    row = lax.broadcasted_iota(jnp.int32, (16, 128), 0) % 4
+    scale = jnp.broadcast_to(scale_ref[0:1, 0:1], (16, 128))
+    for k in range(1, 4):
+        scale = jnp.where(row == k, scale_ref[0:1, k : k + 1], scale)
+    scale = jnp.concatenate([scale] * 8, axis=1)
     total = total * scale
     stack = jnp.concatenate([total[:, c * 128 : c * 128 + 128] for c in range(8)], axis=0)
     grid_ref[...] = column_transform(stack, high_ref, low_ref)
@@ -157,12 +161,12 @@
 ):
     stripe = lax.axis_index("stripe")
     grids = grids_ref[...]
-    modes = mm(forward_ref[...], jnp.concatenate([grids, grids], axis=0), precision=None)
+    modes = mm(forward_ref[...], jnp.concatenate([grids, grids], axis=0))
     prior = prior_ref[...].T
     prior = jnp.concatenate([prior, prior], axis=1)
     modes = modes * jnp.concatenate([prior] * 8, axis=1)
     modes = jnp.concatenate(split(modes), axis=0)
-    back = mm(backward_ref[stripe], modes, precision=None)
+    back = mm(backward_ref[stripe], modes)
     back = back[0:16, :] + back[16:32, :]
     for m in range(8):
         first, second = swap_halves(
@@ -179,7 +183,7 @@
         term = None
         for c in range(4):
             right = kernel_ref[k, :, :, c * 256 : c * 256 + 256].reshape(1024, 256)
-            piece = mm(left[:, c * 256 : c * 256 + 256], right, ((1,), (1,)), precision=None)
+            piece = mm(left[:, c * 256 : c * 256 + 256], right, ((1,), (1,)))
             term = piece if term is None else term + piece
         total = term if k == 0 else jnp.where(freq == k, term, total)
     sub = lax.broadcasted_iota(jnp.int32, (8, 512), 0)
@@ -208,7 +212,7 @@
         blocks.append(total)
     images = jnp.concatenate(blocks, axis=0)
     table = table_ref[lax.axis_index("z"), half]
-    out_ref[...] = mm(table, images, ((0,), (0,)))
+    out_ref[...] = triple_product(table, images)
 
 
 def finish_body(sums_ref, data_ref, noise_ref, out_ref):
@@ -255,8 +259,8 @@
     grids = call(
         adjoint_body,
         jax.ShapeDtypeStruct((8, 16, 1024), bf16),
-        (gathered.reshape(2, 8, 8, 128), kernel, time_spectrum, *columns),
-        (whole(), whole(), scalars(), whole(), whole()),
+        (gathered.reshape(2, 8, 8, 128), kernel, time_spectrum.reshape(1, 4), *columns),
+        (whole(),) * 5,
         (pltpu.VMEM((128, 128), f32),),
         limit=20 << 20,
     )

time: 69.4 us -> 68.7 us (0.990)
  no operation moved by 1% of the time
where the time goes in v7:
time: 68.7 us; the launch traced here: 68.5 us
  blocking collectives  62.1 us (90%)
  Pallas kernels  5.54 us (8%)
  local copies, waits for them, and re-layouts  0.75 us (1%)
    all_to_all x5, blocking collectives, exchange(): return lax.all_to_all(x, axes, 0, 0, tiled=True)  62.1 us
    pallas_call x6, Pallas kernels, call(): pl.pallas_call(body, out_shape=out_shape, in_specs=list(specs), out_specs...  5.54 us

profile of v7, /device:TPU:1, one launch (start us, length us, event | category | flops | bytes accessed | tf_op | source)
XLA Modules:
  0.0 68.5 jit_solution(17764301759849754267)
XLA Ops:
  0.0 0.0 copy-start.6
  0.0 0.7 %copy-done.6 = f32[4,2,64]{2,1,0:T(2,128)S(1)} copy-done((f32[4,2,64]{2,1,0:T(2,128)S(1)}, f32[4,2,64]{2,1,0:T(2,128)}, u32[]{:S(2)}) %copy-start.6) | copy-done | bytes 2072
  0.7 0.0 copy-start.10
  0.7 0.0 slice-start
  0.7 0.1 shard_map.109
  0.8 17.4 %all_to_all.25 = f32[16,4,128]{2,1,0:T(4,128)S(1)} all-to-all(f32[16,4,128]{2,1,0:T(4,128)S(1)} %bitcast.23), channel_id=1, replica_groups=mesh['x_hi'=2,'z'=8,'core'=2,'stripe'=8] {'z','core'}, dimensions={0} | all-to-all | bytes 65536 | tf_op jit(solution)/shard_map/all_to_all | solution.py:229
  18.2 0.0 copy-done.10
  18.2 0.0 copy-start.8
  18.2 0.1 shard_map.110
  18.3 0.0 copy-start.5
  18.4 13.3 %all_to_all.26 = f32[16,8,128]{2,1,0:T(8,128)S(1)} all-to-all(f32[16,8,128]{2,1,0:T(8,128)S(1)} %bitcast.18), channel_id=1, replica_groups=mesh['x_hi'=2,'z'=8,'core'=2,'stripe'=8] {'x_hi','stripe'}, dimensions={0} | all-to-all | bytes 131072 | tf_op jit(solution)/shard_map/all_to_all | solution.py:229
  31.7 0.0 slice-done
  31.7 0.0 slice-done.1
  31.7 0.0 copy-done.2
  31.7 0.0 copy-done.3
  31.7 0.0 copy-done.8
  31.7 0.0 copy-start
  31.7 0.0 copy-start.7
  31.8 0.0 copy-start.9
  31.8 1.5 %shard_map.111 = bf16[8,16,1024]{2,1,0:T(8,128)(2,1)S(1)} custom-call(f32[2,8,8,128]{3,2,1,0:T(8,128)S(1)} %bitcast.16, bf16[4,2,512,1024]{3,2,1,0:T(8,128)(2,1)S(1)} %bitcast.13, f32[1,4]{1,0:T(1,128)S(1)} %bitcast.24, bf16[128,128]{1,0:T(8,128)(2,1)S(1)} %copy-done.3, bf16[128,128]{1,0:T(8,128)(2,1)S(1)} %copy-done.2), custom_call_target="tpu_custom_call" | custom-call | flops 1000000 | bytes 100000 | tf_op jit(solution)/shard_map/pallas_call | solution.py:21
  33.3 8.6 %all_to_all.27 = bf16[8,16,1024]{2,1,0:T(8,128)(2,1)S(1)} all-to-all(bf16[8,16,1024]{2,1,0:T(8,128)(2,1)S(1)} %shard_map.111), channel_id=1, replica_groups=mesh['x_hi'=2,'z'=8,'core'=2,'stripe'=8] {'stripe'}, dimensions={0} | all-to-all | bytes 524288 | tf_op jit(solution)/shard_map/all_to_all | solution.py:229
  41.9 0.0 copy-done.1
  41.9 0.0 copy-done.4
  41.9 0.0 copy-done.5
  41.9 2.9 %shard_map.112 = bf16[4,8,8,128]{3,2,1,0:T(8,128)(2,1)S(1)} custom-call(bf16[128,1024]{1,0:T(8,128)(2,1)S(1)} %bitcast.14, bf16[4,2,512,1024]{3,2,1,0:T(8,128)(2,1)S(1)} %bitcast.13, f32[64,128]{1,0:T(8,128)S(1)} %bitcast.21, bf16[128,256]{1,0:T(8,128)(2,1)S(1)} %copy-done.4, bf16[8,32,256]{2,1,0:T(8,128)(2,1)S(1)} %copy-done.1, ...), custom_call_target="tpu_custom_call" | custom-call | flops 1000000 | bytes 100000 | tf_op jit(solution)/shard_map/pallas_call | solution.py:21
  44.8 13.8 %all_to_all.28 = bf16[32,8,128]{2,1,0:T(8,128)(2,1)S(1)} all-to-all(bf16[32,8,128]{2,1,0:T(8,128)(2,1)S(1)} %bitcast.15), channel_id=1, replica_groups=mesh['x_hi'=2,'z'=8,'core'=2,'stripe'=8] {'x_hi','core','stripe'}, dimensions={0} | all-to-all | bytes 131072 | tf_op jit(solution)/shard_map/all_to_all | solution.py:229
  58.6 0.0 copy-done
  58.6 0.1 shard_map.113
  58.7 9.0 %all_to_all.29 = f32[8,4,128]{2,1,0:T(4,128)S(1)} all-to-all(f32[8,4,128]{2,1,0:T(4,128)S(1)} %bitcast.20), channel_id=1, replica_groups=mesh['x_hi'=2,'z'=8,'core'=2,'stripe'=8] {'z'}, dimensions={0} | all-to-all | bytes 32768 | tf_op jit(solution)/shard_map/all_to_all | solution.py:229
  67.7 0.0 copy-done.7
  67.7 0.0 copy-done.9
  67.7 0.7 %shard_map.114 = f32[4,2,64]{2,1,0:T(2,128)} custom-call(f32[32,128]{1,0:T(8,128)S(1)} %bitcast.19, f32[4,2,64]{2,1,0:T(2,128)S(1)} %copy-done.7, f32[1,64]{1,0:T(1,128)S(1)} %bitcast.25), custom_call_target="tpu_custom_call" | custom-call | flops 1000000 | bytes 100000 | tf_op jit(solution)/shard_map/pallas_call | solution.py:21
  (6 shorter events, 0.0 us)
Async XLA Ops:
  0.0 0.7 %copy-start.6 = (f32[4,2,64]{2,1,0:T(2,128)S(1)}, f32[4,2,64]{2,1,0:T(2,128)}, u32[]{:S(2)}) copy-start(f32[4,2,64]{2,1,0:T(2,128)} %data_ref.3) | copy-start | bytes 6148
  0.7 17.5 %copy-start.10 = (bf16[2,16,16,192]{3,2,1,0:T(8,128)(2,1)S(1)}, bf16[2,16,16,192]{3,2,1,0:T(8,128)(2,1)}, u32[]{:S(2)}) copy-start(bf16[2,16,16,192]{3,2,1,0:T(8,128)(2,1)} %constant.12.clone.table_ref) | copy-start | bytes 589828
  0.7 31.0 %slice-start = ((s8[8388608]{0:T(1024)(128)(4,1)}), s8[4194304]{0:T(1024)(128)(4,1)S(1)}, s32[]{:S(2)}) async-start(s8[8388608]{0:T(1024)(128)(4,1)} %bitcast.12), calls=%async_computation.5 | async-start | bytes 8388608
  18.2 13.5 %slice-start.1 = ((s8[8388608]{0:T(1024)(128)(4,1)}), s8[4194304]{0:T(1024)(128)(4,1)S(1)}, s32[]{:S(2)}) async-start(s8[8388608]{0:T(1024)(128)(4,1)} %bitcast.12), calls=%async_computation.6 | async-start | bytes 8388608
  18.2 13.5 %copy-start.2 = (bf16[128,128]{1,0:T(8,128)(2,1)S(1)}, bf16[128,128]{1,0:T(8,128)(2,1)}, u32[]{:S(2)}) copy-start(bf16[128,128]{1,0:T(8,128)(2,1)} %constant.16.clone.low_ref) | copy-start | bytes 98308
  18.2 13.5 %copy-start.3 = (bf16[128,128]{1,0:T(8,128)(2,1)S(1)}, bf16[128,128]{1,0:T(8,128)(2,1)}, u32[]{:S(2)}) copy-start(bf16[128,128]{1,0:T(8,128)(2,1)} %constant.15.clone.high_ref) | copy-start | bytes 98308
  18.2 13.5 %copy-start.8 = (f32[4]{0:T(128)S(1)}, f32[4]{0:T(128)}, u32[]{:S(2)}) copy-start(f32[4]{0:T(128)} %param.13) | copy-start | bytes 52
  18.3 23.5 %copy-start.1 = (bf16[8,32,256]{2,1,0:T(8,128)(2,1)S(1)}, bf16[8,32,256]{2,1,0:T(8,128)(2,1)}, u32[]{:S(2)}) copy-start(bf16[8,32,256]{2,1,0:T(8,128)(2,1)} %constant.14.clone.backward_ref) | copy-start | bytes 393220
  18.3 23.5 %copy-start.4 = (bf16[128,256]{1,0:T(8,128)(2,1)S(1)}, bf16[128,256]{1,0:T(8,128)(2,1)}, u32[]{:S(2)}) copy-start(bf16[128,256]{1,0:T(8,128)(2,1)} %constant.13.clone.forward_ref) | copy-start | bytes 196612
  18.3 23.5 %copy-start.5 = (f32[128,64]{0,1:T(8,128)S(1)}, f32[128,64]{0,1:T(8,128)}, u32[]{:S(2)}) copy-start(f32[128,64]{0,1:T(8,128)} %param.14) | copy-start | bytes 98308
  31.7 26.9 %copy-start = (bf16[8,4,32,96]{3,2,1,0:T(8,128)(2,1)S(1)}, bf16[8,4,32,96]{3,2,1,0:T(8,128)(2,1)}, u32[]{:S(2)}) copy-start(bf16[8,4,32,96]{3,2,1,0:T(8,128)(2,1)} %constant.17.clone.table_ref) | copy-start | bytes 589828
  31.7 36.0 %copy-start.7 = (f32[4,2,64]{2,1,0:T(2,128)S(1)}, f32[4,2,64]{2,1,0:T(2,128)}, u32[]{:S(2)}) copy-start(f32[4,2,64]{2,1,0:T(2,128)} %data_ref.3) | copy-start | bytes 6148
  31.8 36.0 %copy-start.9 = (f32[64]{0:T(128)S(1)}, f32[64]{0:T(128)}, u32[]{:S(2)}) copy-start(f32[64]{0:T(128)} %param.15) | copy-start | bytes 772

commit v8 on v7

--- a/solution.py
+++ b/solution.py
@@ -157,9 +157,13 @@
 
 
 def images_body(
-    grids_ref, kernel_ref, prior_ref, forward_ref, backward_ref, high_ref, low_ref, out_ref, grid_ref
+    grids_ref, kernel_ref, prior_ref, forward_ref, backward_ref, high_ref, low_ref, out_ref, grid_ref, turned_ref
 ):
     stripe = lax.axis_index("stripe")
+    for row in range(0, 1024, 512):
+        for column in range(0, 1024, 512):
+            tile = kernel_ref[3, row // 512, row % 512 : row % 512 + 512, column : column + 512]
+            turned_ref[column : column + 512, row : row + 512] = tile.T
     grids = grids_ref[...]
     modes = mm(forward_ref[...], jnp.concatenate([grids, grids], axis=0))
     prior = prior_ref[...].T
@@ -180,11 +184,14 @@
     freq = lax.broadcasted_iota(jnp.int32, (16, 1024), 0) % 4
     total = None
     for k in range(4):
-        term = None
-        for c in range(4):
-            right = kernel_ref[k, :, :, c * 256 : c * 256 + 256].reshape(1024, 256)
-            piece = mm(left[:, c * 256 : c * 256 + 256], right, ((1,), (1,)))
-            term = piece if term is None else term + piece
+        if k == 3:
+            term = mm(left, turned_ref[...])
+        else:
+            term = None
+            for c in range(4):
+                right = kernel_ref[k, :, :, c * 256 : c * 256 + 256].reshape(1024, 256)
+                piece = mm(left[:, c * 256 : c * 256 + 256], right, ((1,), (1,)))
+                term = piece if term is None else term + piece
         total = term if k == 0 else jnp.where(freq == k, term, total)
     sub = lax.broadcasted_iota(jnp.int32, (8, 512), 0)
     rows = []
@@ -270,7 +277,7 @@
         jax.ShapeDtypeStruct((4, 8, 8, 128), bf16),
         (grids, kernel, prior_spectrum.T, forward, backward, *columns),
         (whole(),) * 7,
-        (pltpu.VMEM((128, 128), f32),),
+        (pltpu.VMEM((128, 128), f32), pltpu.VMEM((1024, 1024), bf16)),
         limit=20 << 20,
     )
     images = exchange(images.reshape(32, 8, 128), ("x_hi", "core", "stripe"))

time: 68.7 us -> 68.5 us (level)
  no operation moved by 1% of the time
where the time goes in v8:
time: 68.5 us; the launch traced here: 68.2 us
  blocking collectives  62.1 us (91%)
  Pallas kernels  5.29 us (8%)
  local copies, waits for them, and re-layouts  0.75 us (1%)
    all_to_all x5, blocking collectives, exchange(): return lax.all_to_all(x, axes, 0, 0, tiled=True)  62.1 us
    pallas_call x6, Pallas kernels, call(): pl.pallas_call(body, out_shape=out_shape, in_specs=list(specs), out_specs...  5.29 us

profile of v8, /device:TPU:1, one launch (start us, length us, event | category | flops | bytes accessed | tf_op | source)
XLA Modules:
  0.0 68.2 jit_solution(11743566024245760423)
XLA Ops:
  0.0 0.0 copy-start.6
  0.0 0.7 %copy-done.6 = f32[4,2,64]{2,1,0:T(2,128)S(1)} copy-done((f32[4,2,64]{2,1,0:T(2,128)S(1)}, f32[4,2,64]{2,1,0:T(2,128)}, u32[]{:S(2)}) %copy-start.6) | copy-done | bytes 2072
  0.7 0.0 copy-start.10
  0.7 0.0 slice-start
  0.7 0.1 shard_map.109
  0.8 17.4 %all_to_all.25 = f32[16,4,128]{2,1,0:T(4,128)S(1)} all-to-all(f32[16,4,128]{2,1,0:T(4,128)S(1)} %bitcast.23), channel_id=1, replica_groups=mesh['x_hi'=2,'z'=8,'core'=2,'stripe'=8] {'z','core'}, dimensions={0} | all-to-all | bytes 65536 | tf_op jit(solution)/shard_map/all_to_all | solution.py:236
  18.2 0.0 copy-done.10
  18.2 0.0 copy-start.8
  18.2 0.1 shard_map.110
  18.3 0.0 copy-start.5
  18.4 13.3 %all_to_all.26 = f32[16,8,128]{2,1,0:T(8,128)S(1)} all-to-all(f32[16,8,128]{2,1,0:T(8,128)S(1)} %bitcast.18), channel_id=1, replica_groups=mesh['x_hi'=2,'z'=8,'core'=2,'stripe'=8] {'x_hi','stripe'}, dimensions={0} | all-to-all | bytes 131072 | tf_op jit(solution)/shard_map/all_to_all | solution.py:236
  31.7 0.0 slice-done
  31.7 0.0 slice-done.1
  31.7 0.0 copy-done.2
  31.7 0.0 copy-done.3
  31.7 0.0 copy-done.8
  31.7 0.0 copy-start
  31.7 0.0 copy-start.7
  31.8 0.0 copy-start.9
  31.8 1.5 %shard_map.111 = bf16[8,16,1024]{2,1,0:T(8,128)(2,1)S(1)} custom-call(f32[2,8,8,128]{3,2,1,0:T(8,128)S(1)} %bitcast.16, bf16[4,2,512,1024]{3,2,1,0:T(8,128)(2,1)S(1)} %bitcast.13, f32[1,4]{1,0:T(1,128)S(1)} %bitcast.24, bf16[128,128]{1,0:T(8,128)(2,1)S(1)} %copy-done.3, bf16[128,128]{1,0:T(8,128)(2,1)S(1)} %copy-done.2), custom_call_target="tpu_custom_call" | custom-call | flops 1000000 | bytes 100000 | tf_op jit(solution)/shard_map/pallas_call | solution.py:21
  33.3 8.6 %all_to_all.27 = bf16[8,16,1024]{2,1,0:T(8,128)(2,1)S(1)} all-to-all(bf16[8,16,1024]{2,1,0:T(8,128)(2,1)S(1)} %shard_map.111), channel_id=1, replica_groups=mesh['x_hi'=2,'z'=8,'core'=2,'stripe'=8] {'stripe'}, dimensions={0} | all-to-all | bytes 524288 | tf_op jit(solution)/shard_map/all_to_all | solution.py:236
  41.9 0.0 copy-done.1
  41.9 0.0 copy-done.4
  41.9 0.0 copy-done.5
  41.9 2.7 %shard_map.112 = bf16[4,8,8,128]{3,2,1,0:T(8,128)(2,1)S(1)} custom-call(bf16[128,1024]{1,0:T(8,128)(2,1)S(1)} %bitcast.14, bf16[4,2,512,1024]{3,2,1,0:T(8,128)(2,1)S(1)} %bitcast.13, f32[64,128]{1,0:T(8,128)S(1)} %bitcast.21, bf16[128,256]{1,0:T(8,128)(2,1)S(1)} %copy-done.4, bf16[8,32,256]{2,1,0:T(8,128)(2,1)S(1)} %copy-done.1, ...), custom_call_target="tpu_custom_call" | custom-call | flops 1000000 | bytes 100000 | tf_op jit(solution)/shard_map/pallas_call | solution.py:21
  44.5 13.8 %all_to_all.28 = bf16[32,8,128]{2,1,0:T(8,128)(2,1)S(1)} all-to-all(bf16[32,8,128]{2,1,0:T(8,128)(2,1)S(1)} %bitcast.15), channel_id=1, replica_groups=mesh['x_hi'=2,'z'=8,'core'=2,'stripe'=8] {'x_hi','core','stripe'}, dimensions={0} | all-to-all | bytes 131072 | tf_op jit(solution)/shard_map/all_to_all | solution.py:236
  58.3 0.0 copy-done
  58.3 0.1 shard_map.113
  58.5 9.0 %all_to_all.29 = f32[8,4,128]{2,1,0:T(4,128)S(1)} all-to-all(f32[8,4,128]{2,1,0:T(4,128)S(1)} %bitcast.20), channel_id=1, replica_groups=mesh['x_hi'=2,'z'=8,'core'=2,'stripe'=8] {'z'}, dimensions={0} | all-to-all | bytes 32768 | tf_op jit(solution)/shard_map/all_to_all | solution.py:236
  67.5 0.0 copy-done.7
  67.5 0.0 copy-done.9
  67.5 0.7 %shard_map.114 = f32[4,2,64]{2,1,0:T(2,128)} custom-call(f32[32,128]{1,0:T(8,128)S(1)} %bitcast.19, f32[4,2,64]{2,1,0:T(2,128)S(1)} %copy-done.7, f32[1,64]{1,0:T(1,128)S(1)} %bitcast.25), custom_call_target="tpu_custom_call" | custom-call | flops 1000000 | bytes 100000 | tf_op jit(solution)/shard_map/pallas_call | solution.py:21
  (6 shorter events, 0.0 us)
Async XLA Ops:
  0.0 0.7 %copy-start.6 = (f32[4,2,64]{2,1,0:T(2,128)S(1)}, f32[4,2,64]{2,1,0:T(2,128)}, u32[]{:S(2)}) copy-start(f32[4,2,64]{2,1,0:T(2,128)} %data_ref.3) | copy-start | bytes 6148
  0.7 17.5 %copy-start.10 = (bf16[2,16,16,192]{3,2,1,0:T(8,128)(2,1)S(1)}, bf16[2,16,16,192]{3,2,1,0:T(8,128)(2,1)}, u32[]{:S(2)}) copy-start(bf16[2,16,16,192]{3,2,1,0:T(8,128)(2,1)} %constant.12.clone.table_ref) | copy-start | bytes 589828
  0.7 31.0 %slice-start = ((s8[8388608]{0:T(1024)(128)(4,1)}), s8[4194304]{0:T(1024)(128)(4,1)S(1)}, s32[]{:S(2)}) async-start(s8[8388608]{0:T(1024)(128)(4,1)} %bitcast.12), calls=%async_computation.5 | async-start | bytes 8388608
  18.2 13.5 %slice-start.1 = ((s8[8388608]{0:T(1024)(128)(4,1)}), s8[4194304]{0:T(1024)(128)(4,1)S(1)}, s32[]{:S(2)}) async-start(s8[8388608]{0:T(1024)(128)(4,1)} %bitcast.12), calls=%async_computation.6 | async-start | bytes 8388608
  18.2 13.5 %copy-start.2 = (bf16[128,128]{1,0:T(8,128)(2,1)S(1)}, bf16[128,128]{1,0:T(8,128)(2,1)}, u32[]{:S(2)}) copy-start(bf16[128,128]{1,0:T(8,128)(2,1)} %constant.16.clone.low_ref) | copy-start | bytes 98308
  18.2 13.5 %copy-start.3 = (bf16[128,128]{1,0:T(8,128)(2,1)S(1)}, bf16[128,128]{1,0:T(8,128)(2,1)}, u32[]{:S(2)}) copy-start(bf16[128,128]{1,0:T(8,128)(2,1)} %constant.15.clone.high_ref) | copy-start | bytes 98308
  18.2 13.5 %copy-start.8 = (f32[4]{0:T(128)S(1)}, f32[4]{0:T(128)}, u32[]{:S(2)}) copy-start(f32[4]{0:T(128)} %param.13) | copy-start | bytes 52
  18.3 23.5 %copy-start.1 = (bf16[8,32,256]{2,1,0:T(8,128)(2,1)S(1)}, bf16[8,32,256]{2,1,0:T(8,128)(2,1)}, u32[]{:S(2)}) copy-start(bf16[8,32,256]{2,1,0:T(8,128)(2,1)} %constant.14.clone.backward_ref) | copy-start | bytes 393220
  18.3 23.5 %copy-start.4 = (bf16[128,256]{1,0:T(8,128)(2,1)S(1)}, bf16[128,256]{1,0:T(8,128)(2,1)}, u32[]{:S(2)}) copy-start(bf16[128,256]{1,0:T(8,128)(2,1)} %constant.13.clone.forward_ref) | copy-start | bytes 196612
  18.3 23.5 %copy-start.5 = (f32[128,64]{0,1:T(8,128)S(1)}, f32[128,64]{0,1:T(8,128)}, u32[]{:S(2)}) copy-start(f32[128,64]{0,1:T(8,128)} %param.14) | copy-start | bytes 98308
  31.7 26.6 %copy-start = (bf16[8,4,32,96]{3,2,1,0:T(8,128)(2,1)S(1)}, bf16[8,4,32,96]{3,2,1,0:T(8,128)(2,1)}, u32[]{:S(2)}) copy-start(bf16[8,4,32,96]{3,2,1,0:T(8,128)(2,1)} %constant.17.clone.table_ref) | copy-start | bytes 589828
  31.7 35.7 %copy-start.7 = (f32[4,2,64]{2,1,0:T(2,128)S(1)}, f32[4,2,64]{2,1,0:T(2,128)}, u32[]{:S(2)}) copy-start(f32[4,2,64]{2,1,0:T(2,128)} %data_ref.3) | copy-start | bytes 6148
  31.8 35.7 %copy-start.9 = (f32[64]{0:T(128)S(1)}, f32[64]{0:T(128)}, u32[]{:S(2)}) copy-start(f32[64]{0:T(128)} %param.15) | copy-start | bytes 772

commit v9 on v8

--- a/solution.py
+++ b/solution.py
@@ -160,10 +160,10 @@
     grids_ref, kernel_ref, prior_ref, forward_ref, backward_ref, high_ref, low_ref, out_ref, grid_ref, turned_ref
 ):
     stripe = lax.axis_index("stripe")
-    for row in range(0, 1024, 512):
+    for c in range(3):
         for column in range(0, 1024, 512):
-            tile = kernel_ref[3, row // 512, row % 512 : row % 512 + 512, column : column + 512]
-            turned_ref[column : column + 512, row : row + 512] = tile.T
+            tile = kernel_ref[(c + 5) // 2, (c + 1) % 2, :, column : column + 512]
+            turned_ref[column : column + 512, c * 512 : c * 512 + 512] = tile.T
     grids = grids_ref[...]
     modes = mm(forward_ref[...], jnp.concatenate([grids, grids], axis=0))
     prior = prior_ref[...].T
@@ -185,7 +185,14 @@
     total = None
     for k in range(4):
         if k == 3:
-            term = mm(left, turned_ref[...])
+            term = mm(left, turned_ref[:, 512:])
+        elif k == 2:
+            term = None
+            for c in range(4):
+                right = kernel_ref[k, 0, :, c * 256 : c * 256 + 256]
+                piece = mm(left[:, c * 256 : c * 256 + 256], right, ((1,), (1,)))
+                term = piece if term is None else term + piece
+            term = jnp.concatenate([term, mm(left, turned_ref[:, :512])], axis=1)
         else:
             term = None
             for c in range(4):
@@ -277,7 +284,7 @@
         jax.ShapeDtypeStruct((4, 8, 8, 128), bf16),
         (grids, kernel, prior_spectrum.T, forward, backward, *columns),
         (whole(),) * 7,
-        (pltpu.VMEM((128, 128), f32), pltpu.VMEM((1024, 1024), bf16)),
+        (pltpu.VMEM((128, 128), f32), pltpu.VMEM((1024, 1536), bf16)),
         limit=20 << 20,
     )
     images = exchange(images.reshape(32, 8, 128), ("x_hi", "core", "stripe"))

time: 68.5 us -> 68.3 us (level)
  no operation moved by 1% of the time
where the time goes in v9:
time: 68.3 us; the launch traced here: 68.1 us
  blocking collectives  62.1 us (91%)
  Pallas kernels  5.16 us (8%)
  local copies, waits for them, and re-layouts  0.75 us (1%)
    all_to_all x5, blocking collectives, exchange(): return lax.all_to_all(x, axes, 0, 0, tiled=True)  62.1 us
    pallas_call x6, Pallas kernels, call(): pl.pallas_call(body, out_shape=out_shape, in_specs=list(specs), out_specs...  5.16 us

profile of v9, /device:TPU:1, one launch (start us, length us, event | category | flops | bytes accessed | tf_op | source)
XLA Modules:
  0.0 68.1 jit_solution(17258031196776812866)
XLA Ops:
  0.0 0.0 copy-start.6
  0.0 0.7 %copy-done.6 = f32[4,2,64]{2,1,0:T(2,128)S(1)} copy-done((f32[4,2,64]{2,1,0:T(2,128)S(1)}, f32[4,2,64]{2,1,0:T(2,128)}, u32[]{:S(2)}) %copy-start.6) | copy-done | bytes 2072
  0.7 0.0 copy-start.10
  0.7 0.0 slice-start
  0.7 0.1 shard_map.109
  0.8 17.4 %all_to_all.25 = f32[16,4,128]{2,1,0:T(4,128)S(1)} all-to-all(f32[16,4,128]{2,1,0:T(4,128)S(1)} %bitcast.23), channel_id=1, replica_groups=mesh['x_hi'=2,'z'=8,'core'=2,'stripe'=8] {'z','core'}, dimensions={0} | all-to-all | bytes 65536 | tf_op jit(solution)/shard_map/all_to_all | solution.py:243
  18.2 0.0 copy-done.10
  18.2 0.0 copy-start.8
  18.2 0.1 shard_map.110
  18.3 0.0 copy-start.5
  18.4 13.3 %all_to_all.26 = f32[16,8,128]{2,1,0:T(8,128)S(1)} all-to-all(f32[16,8,128]{2,1,0:T(8,128)S(1)} %bitcast.18), channel_id=1, replica_groups=mesh['x_hi'=2,'z'=8,'core'=2,'stripe'=8] {'x_hi','stripe'}, dimensions={0} | all-to-all | bytes 131072 | tf_op jit(solution)/shard_map/all_to_all | solution.py:243
  31.7 0.0 slice-done
  31.7 0.0 slice-done.1
  31.7 0.0 copy-done.2
  31.7 0.0 copy-done.3
  31.7 0.0 copy-done.8
  31.7 0.0 copy-start
  31.7 0.0 copy-start.7
  31.8 0.0 copy-start.9
  31.8 1.5 %shard_map.111 = bf16[8,16,1024]{2,1,0:T(8,128)(2,1)S(1)} custom-call(f32[2,8,8,128]{3,2,1,0:T(8,128)S(1)} %bitcast.16, bf16[4,2,512,1024]{3,2,1,0:T(8,128)(2,1)S(1)} %bitcast.13, f32[1,4]{1,0:T(1,128)S(1)} %bitcast.24, bf16[128,128]{1,0:T(8,128)(2,1)S(1)} %copy-done.3, bf16[128,128]{1,0:T(8,128)(2,1)S(1)} %copy-done.2), custom_call_target="tpu_custom_call" | custom-call | flops 1000000 | bytes 100000 | tf_op jit(solution)/shard_map/pallas_call | solution.py:21
  33.3 8.6 %all_to_all.27 = bf16[8,16,1024]{2,1,0:T(8,128)(2,1)S(1)} all-to-all(bf16[8,16,1024]{2,1,0:T(8,128)(2,1)S(1)} %shard_map.111), channel_id=1, replica_groups=mesh['x_hi'=2,'z'=8,'core'=2,'stripe'=8] {'stripe'}, dimensions={0} | all-to-all | bytes 524288 | tf_op jit(solution)/shard_map/all_to_all | solution.py:243
  41.9 0.0 copy-done.1
  41.9 0.0 copy-done.4
  41.9 0.0 copy-done.5
  41.9 2.5 %shard_map.112 = bf16[4,8,8,128]{3,2,1,0:T(8,128)(2,1)S(1)} custom-call(bf16[128,1024]{1,0:T(8,128)(2,1)S(1)} %bitcast.14, bf16[4,2,512,1024]{3,2,1,0:T(8,128)(2,1)S(1)} %bitcast.13, f32[64,128]{1,0:T(8,128)S(1)} %bitcast.21, bf16[128,256]{1,0:T(8,128)(2,1)S(1)} %copy-done.4, bf16[8,32,256]{2,1,0:T(8,128)(2,1)S(1)} %copy-done.1, ...), custom_call_target="tpu_custom_call" | custom-call | flops 1000000 | bytes 100000 | tf_op jit(solution)/shard_map/pallas_call | solution.py:21
  44.4 13.8 %all_to_all.28 = bf16[32,8,128]{2,1,0:T(8,128)(2,1)S(1)} all-to-all(bf16[32,8,128]{2,1,0:T(8,128)(2,1)S(1)} %bitcast.15), channel_id=1, replica_groups=mesh['x_hi'=2,'z'=8,'core'=2,'stripe'=8] {'x_hi','core','stripe'}, dimensions={0} | all-to-all | bytes 131072 | tf_op jit(solution)/shard_map/all_to_all | solution.py:243
  58.2 0.0 copy-done
  58.2 0.1 shard_map.113
  58.4 9.0 %all_to_all.29 = f32[8,4,128]{2,1,0:T(4,128)S(1)} all-to-all(f32[8,4,128]{2,1,0:T(4,128)S(1)} %bitcast.20), channel_id=1, replica_groups=mesh['x_hi'=2,'z'=8,'core'=2,'stripe'=8] {'z'}, dimensions={0} | all-to-all | bytes 32768 | tf_op jit(solution)/shard_map/all_to_all | solution.py:243
  67.3 0.0 copy-done.7
  67.3 0.0 copy-done.9
  67.3 0.7 %shard_map.114 = f32[4,2,64]{2,1,0:T(2,128)} custom-call(f32[32,128]{1,0:T(8,128)S(1)} %bitcast.19, f32[4,2,64]{2,1,0:T(2,128)S(1)} %copy-done.7, f32[1,64]{1,0:T(1,128)S(1)} %bitcast.25), custom_call_target="tpu_custom_call" | custom-call | flops 1000000 | bytes 100000 | tf_op jit(solution)/shard_map/pallas_call | solution.py:21
  (6 shorter events, 0.0 us)
Async XLA Ops:
  0.0 0.7 %copy-start.6 = (f32[4,2,64]{2,1,0:T(2,128)S(1)}, f32[4,2,64]{2,1,0:T(2,128)}, u32[]{:S(2)}) copy-start(f32[4,2,64]{2,1,0:T(2,128)} %data_ref.3) | copy-start | bytes 6148
  0.7 17.5 %copy-start.10 = (bf16[2,16,16,192]{3,2,1,0:T(8,128)(2,1)S(1)}, bf16[2,16,16,192]{3,2,1,0:T(8,128)(2,1)}, u32[]{:S(2)}) copy-start(bf16[2,16,16,192]{3,2,1,0:T(8,128)(2,1)} %constant.12.clone.table_ref) | copy-start | bytes 589828
  0.7 31.0 %slice-start = ((s8[8388608]{0:T(1024)(128)(4,1)}), s8[4194304]{0:T(1024)(128)(4,1)S(1)}, s32[]{:S(2)}) async-start(s8[8388608]{0:T(1024)(128)(4,1)} %bitcast.12), calls=%async_computation.5 | async-start | bytes 8388608
  18.2 13.5 %slice-start.1 = ((s8[8388608]{0:T(1024)(128)(4,1)}), s8[4194304]{0:T(1024)(128)(4,1)S(1)}, s32[]{:S(2)}) async-start(s8[8388608]{0:T(1024)(128)(4,1)} %bitcast.12), calls=%async_computation.6 | async-start | bytes 8388608
  18.2 13.5 %copy-start.2 = (bf16[128,128]{1,0:T(8,128)(2,1)S(1)}, bf16[128,128]{1,0:T(8,128)(2,1)}, u32[]{:S(2)}) copy-start(bf16[128,128]{1,0:T(8,128)(2,1)} %constant.16.clone.low_ref) | copy-start | bytes 98308
  18.2 13.5 %copy-start.3 = (bf16[128,128]{1,0:T(8,128)(2,1)S(1)}, bf16[128,128]{1,0:T(8,128)(2,1)}, u32[]{:S(2)}) copy-start(bf16[128,128]{1,0:T(8,128)(2,1)} %constant.15.clone.high_ref) | copy-start | bytes 98308
  18.2 13.5 %copy-start.8 = (f32[4]{0:T(128)S(1)}, f32[4]{0:T(128)}, u32[]{:S(2)}) copy-start(f32[4]{0:T(128)} %param.13) | copy-start | bytes 52
  18.3 23.5 %copy-start.1 = (bf16[8,32,256]{2,1,0:T(8,128)(2,1)S(1)}, bf16[8,32,256]{2,1,0:T(8,128)(2,1)}, u32[]{:S(2)}) copy-start(bf16[8,32,256]{2,1,0:T(8,128)(2,1)} %constant.14.clone.backward_ref) | copy-start | bytes 393220
  18.3 23.5 %copy-start.4 = (bf16[128,256]{1,0:T(8,128)(2,1)S(1)}, bf16[128,256]{1,0:T(8,128)(2,1)}, u32[]{:S(2)}) copy-start(bf16[128,256]{1,0:T(8,128)(2,1)} %constant.13.clone.forward_ref) | copy-start | bytes 196612
  18.3 23.5 %copy-start.5 = (f32[128,64]{0,1:T(8,128)S(1)}, f32[128,64]{0,1:T(8,128)}, u32[]{:S(2)}) copy-start(f32[128,64]{0,1:T(8,128)} %param.14) | copy-start | bytes 98308
  31.7 26.5 %copy-start = (bf16[8,4,32,96]{3,2,1,0:T(8,128)(2,1)S(1)}, bf16[8,4,32,96]{3,2,1,0:T(8,128)(2,1)}, u32[]{:S(2)}) copy-start(bf16[8,4,32,96]{3,2,1,0:T(8,128)(2,1)} %constant.17.clone.table_ref) | copy-start | bytes 589828
  31.7 35.6 %copy-start.7 = (f32[4,2,64]{2,1,0:T(2,128)S(1)}, f32[4,2,64]{2,1,0:T(2,128)}, u32[]{:S(2)}) copy-start(f32[4,2,64]{2,1,0:T(2,128)} %data_ref.3) | copy-start | bytes 6148
  31.8 35.6 %copy-start.9 = (f32[64]{0:T(128)S(1)}, f32[64]{0:T(128)}, u32[]{:S(2)}) copy-start(f32[64]{0:T(128)} %param.15) | copy-start | bytes 772

commit v10 on v8

--- a/solution.py
+++ b/solution.py
@@ -160,10 +160,11 @@
     grids_ref, kernel_ref, prior_ref, forward_ref, backward_ref, high_ref, low_ref, out_ref, grid_ref, turned_ref
 ):
     stripe = lax.axis_index("stripe")
-    for row in range(0, 1024, 512):
-        for column in range(0, 1024, 512):
-            tile = kernel_ref[3, row // 512, row % 512 : row % 512 + 512, column : column + 512]
-            turned_ref[column : column + 512, row : row + 512] = tile.T
+    for k in range(2, 4):
+        for c in range(2):
+            for column in range(0, 1024, 512):
+                tile = kernel_ref[k, c, :, column : column + 512]
+                turned_ref[k - 2, column : column + 512, c * 512 : c * 512 + 512] = tile.T
     grids = grids_ref[...]
     modes = mm(forward_ref[...], jnp.concatenate([grids, grids], axis=0))
     prior = prior_ref[...].T
@@ -184,8 +185,8 @@
     freq = lax.broadcasted_iota(jnp.int32, (16, 1024), 0) % 4
     total = None
     for k in range(4):
-        if k == 3:
-            term = mm(left, turned_ref[...])
+        if k >= 2:
+            term = mm(left, turned_ref[k - 2])
         else:
             term = None
             for c in range(4):
@@ -277,7 +278,7 @@
         jax.ShapeDtypeStruct((4, 8, 8, 128), bf16),
         (grids, kernel, prior_spectrum.T, forward, backward, *columns),
         (whole(),) * 7,
-        (pltpu.VMEM((128, 128), f32), pltpu.VMEM((1024, 1024), bf16)),
+        (pltpu.VMEM((128, 128), f32), pltpu.VMEM((2, 1024, 1024), bf16)),
         limit=20 << 20,
     )
     images = exchange(images.reshape(32, 8, 128), ("x_hi", "core", "stripe"))

time: 68.5 us -> 68.2 us (level)
  no operation moved by 1% of the time
where the time goes in v10:
time: 68.2 us; the launch traced here: 67.9 us
  blocking collectives  62.1 us (91%)
  Pallas kernels  5.03 us (7%)
  local copies, waits for them, and re-layouts  0.75 us (1%)
    all_to_all x5, blocking collectives, exchange(): return lax.all_to_all(x, axes, 0, 0, tiled=True)  62.1 us
    pallas_call x6, Pallas kernels, call(): pl.pallas_call(body, out_shape=out_shape, in_specs=list(specs), out_specs...  5.03 us

profile of v10, /device:TPU:1, one launch (start us, length us, event | category | flops | bytes accessed | tf_op | source)
XLA Modules:
  0.0 67.9 jit_solution(6792884439438783784)
XLA Ops:
  0.0 0.0 copy-start.6
  0.0 0.7 %copy-done.6 = f32[4,2,64]{2,1,0:T(2,128)S(1)} copy-done((f32[4,2,64]{2,1,0:T(2,128)S(1)}, f32[4,2,64]{2,1,0:T(2,128)}, u32[]{:S(2)}) %copy-start.6) | copy-done | bytes 2072
  0.7 0.0 copy-start.10
  0.7 0.0 slice-start
  0.7 0.1 shard_map.109
  0.8 17.4 %all_to_all.25 = f32[16,4,128]{2,1,0:T(4,128)S(1)} all-to-all(f32[16,4,128]{2,1,0:T(4,128)S(1)} %bitcast.23), channel_id=1, replica_groups=mesh['x_hi'=2,'z'=8,'core'=2,'stripe'=8] {'z','core'}, dimensions={0} | all-to-all | bytes 65536 | tf_op jit(solution)/shard_map/all_to_all | solution.py:237
  18.2 0.0 copy-done.10
  18.2 0.0 copy-start.8
  18.2 0.1 shard_map.110
  18.3 0.0 copy-start.5
  18.4 13.3 %all_to_all.26 = f32[16,8,128]{2,1,0:T(8,128)S(1)} all-to-all(f32[16,8,128]{2,1,0:T(8,128)S(1)} %bitcast.18), channel_id=1, replica_groups=mesh['x_hi'=2,'z'=8,'core'=2,'stripe'=8] {'x_hi','stripe'}, dimensions={0} | all-to-all | bytes 131072 | tf_op jit(solution)/shard_map/all_to_all | solution.py:237
  31.7 0.0 slice-done
  31.7 0.0 slice-done.1
  31.7 0.0 copy-done.2
  31.7 0.0 copy-done.3
  31.7 0.0 copy-done.8
  31.7 0.0 copy-start
  31.7 0.0 copy-start.7
  31.8 0.0 copy-start.9
  31.8 1.5 %shard_map.111 = bf16[8,16,1024]{2,1,0:T(8,128)(2,1)S(1)} custom-call(f32[2,8,8,128]{3,2,1,0:T(8,128)S(1)} %bitcast.16, bf16[4,2,512,1024]{3,2,1,0:T(8,128)(2,1)S(1)} %bitcast.13, f32[1,4]{1,0:T(1,128)S(1)} %bitcast.24, bf16[128,128]{1,0:T(8,128)(2,1)S(1)} %copy-done.3, bf16[128,128]{1,0:T(8,128)(2,1)S(1)} %copy-done.2), custom_call_target="tpu_custom_call" | custom-call | flops 1000000 | bytes 100000 | tf_op jit(solution)/shard_map/pallas_call | solution.py:21
  33.3 8.6 %all_to_all.27 = bf16[8,16,1024]{2,1,0:T(8,128)(2,1)S(1)} all-to-all(bf16[8,16,1024]{2,1,0:T(8,128)(2,1)S(1)} %shard_map.111), channel_id=1, replica_groups=mesh['x_hi'=2,'z'=8,'core'=2,'stripe'=8] {'stripe'}, dimensions={0} | all-to-all | bytes 524288 | tf_op jit(solution)/shard_map/all_to_all | solution.py:237
  41.9 0.0 copy-done.1
  41.9 0.0 copy-done.4
  41.9 0.0 copy-done.5
  41.9 2.4 %shard_map.112 = bf16[4,8,8,128]{3,2,1,0:T(8,128)(2,1)S(1)} custom-call(bf16[128,1024]{1,0:T(8,128)(2,1)S(1)} %bitcast.14, bf16[4,2,512,1024]{3,2,1,0:T(8,128)(2,1)S(1)} %bitcast.13, f32[64,128]{1,0:T(8,128)S(1)} %bitcast.21, bf16[128,256]{1,0:T(8,128)(2,1)S(1)} %copy-done.4, bf16[8,32,256]{2,1,0:T(8,128)(2,1)S(1)} %copy-done.1, ...), custom_call_target="tpu_custom_call" | custom-call | flops 1000000 | bytes 100000 | tf_op jit(solution)/shard_map/pallas_call | solution.py:21
  44.3 13.8 %all_to_all.28 = bf16[32,8,128]{2,1,0:T(8,128)(2,1)S(1)} all-to-all(bf16[32,8,128]{2,1,0:T(8,128)(2,1)S(1)} %bitcast.15), channel_id=1, replica_groups=mesh['x_hi'=2,'z'=8,'core'=2,'stripe'=8] {'x_hi','core','stripe'}, dimensions={0} | all-to-all | bytes 131072 | tf_op jit(solution)/shard_map/all_to_all | solution.py:237
  58.1 0.0 copy-done
  58.1 0.1 shard_map.113
  58.2 9.0 %all_to_all.29 = f32[8,4,128]{2,1,0:T(4,128)S(1)} all-to-all(f32[8,4,128]{2,1,0:T(4,128)S(1)} %bitcast.20), channel_id=1, replica_groups=mesh['x_hi'=2,'z'=8,'core'=2,'stripe'=8] {'z'}, dimensions={0} | all-to-all | bytes 32768 | tf_op jit(solution)/shard_map/all_to_all | solution.py:237
  67.2 0.0 copy-done.7
  67.2 0.0 copy-done.9
  67.2 0.7 %shard_map.114 = f32[4,2,64]{2,1,0:T(2,128)} custom-call(f32[32,128]{1,0:T(8,128)S(1)} %bitcast.19, f32[4,2,64]{2,1,0:T(2,128)S(1)} %copy-done.7, f32[1,64]{1,0:T(1,128)S(1)} %bitcast.25), custom_call_target="tpu_custom_call" | custom-call | flops 1000000 | bytes 100000 | tf_op jit(solution)/shard_map/pallas_call | solution.py:21
  (6 shorter events, 0.0 us)
Async XLA Ops:
  0.0 0.7 %copy-start.6 = (f32[4,2,64]{2,1,0:T(2,128)S(1)}, f32[4,2,64]{2,1,0:T(2,128)}, u32[]{:S(2)}) copy-start(f32[4,2,64]{2,1,0:T(2,128)} %data_ref.3) | copy-start | bytes 6148
  0.7 17.5 %copy-start.10 = (bf16[2,16,16,192]{3,2,1,0:T(8,128)(2,1)S(1)}, bf16[2,16,16,192]{3,2,1,0:T(8,128)(2,1)}, u32[]{:S(2)}) copy-start(bf16[2,16,16,192]{3,2,1,0:T(8,128)(2,1)} %constant.12.clone.table_ref) | copy-start | bytes 589828
  0.7 31.0 %slice-start = ((s8[8388608]{0:T(1024)(128)(4,1)}), s8[4194304]{0:T(1024)(128)(4,1)S(1)}, s32[]{:S(2)}) async-start(s8[8388608]{0:T(1024)(128)(4,1)} %bitcast.12), calls=%async_computation.5 | async-start | bytes 8388608
  18.2 13.5 %slice-start.1 = ((s8[8388608]{0:T(1024)(128)(4,1)}), s8[4194304]{0:T(1024)(128)(4,1)S(1)}, s32[]{:S(2)}) async-start(s8[8388608]{0:T(1024)(128)(4,1)} %bitcast.12), calls=%async_computation.6 | async-start | bytes 8388608
  18.2 13.5 %copy-start.2 = (bf16[128,128]{1,0:T(8,128)(2,1)S(1)}, bf16[128,128]{1,0:T(8,128)(2,1)}, u32[]{:S(2)}) copy-start(bf16[128,128]{1,0:T(8,128)(2,1)} %constant.16.clone.low_ref) | copy-start | bytes 98308
  18.2 13.5 %copy-start.3 = (bf16[128,128]{1,0:T(8,128)(2,1)S(1)}, bf16[128,128]{1,0:T(8,128)(2,1)}, u32[]{:S(2)}) copy-start(bf16[128,128]{1,0:T(8,128)(2,1)} %constant.15.clone.high_ref) | copy-start | bytes 98308
  18.2 13.5 %copy-start.8 = (f32[4]{0:T(128)S(1)}, f32[4]{0:T(128)}, u32[]{:S(2)}) copy-start(f32[4]{0:T(128)} %param.13) | copy-start | bytes 52
  18.3 23.5 %copy-start.1 = (bf16[8,32,256]{2,1,0:T(8,128)(2,1)S(1)}, bf16[8,32,256]{2,1,0:T(8,128)(2,1)}, u32[]{:S(2)}) copy-start(bf16[8,32,256]{2,1,0:T(8,128)(2,1)} %constant.14.clone.backward_ref) | copy-start | bytes 393220
  18.3 23.5 %copy-start.4 = (bf16[128,256]{1,0:T(8,128)(2,1)S(1)}, bf16[128,256]{1,0:T(8,128)(2,1)}, u32[]{:S(2)}) copy-start(bf16[128,256]{1,0:T(8,128)(2,1)} %constant.13.clone.forward_ref) | copy-start | bytes 196612
  18.3 23.5 %copy-start.5 = (f32[128,64]{0,1:T(8,128)S(1)}, f32[128,64]{0,1:T(8,128)}, u32[]{:S(2)}) copy-start(f32[128,64]{0,1:T(8,128)} %param.14) | copy-start | bytes 98308
  31.7 26.4 %copy-start = (bf16[8,4,32,96]{3,2,1,0:T(8,128)(2,1)S(1)}, bf16[8,4,32,96]{3,2,1,0:T(8,128)(2,1)}, u32[]{:S(2)}) copy-start(bf16[8,4,32,96]{3,2,1,0:T(8,128)(2,1)} %constant.17.clone.table_ref) | copy-start | bytes 589828
  31.7 35.5 %copy-start.7 = (f32[4,2,64]{2,1,0:T(2,128)S(1)}, f32[4,2,64]{2,1,0:T(2,128)}, u32[]{:S(2)}) copy-start(f32[4,2,64]{2,1,0:T(2,128)} %data_ref.3) | copy-start | bytes 6148
  31.8 35.4 %copy-start.9 = (f32[64]{0:T(128)S(1)}, f32[64]{0:T(128)}, u32[]{:S(2)}) copy-start(f32[64]{0:T(128)} %param.15) | copy-start | bytes 772

commit v11 on v10

--- a/solution.py
+++ b/solution.py
@@ -160,11 +160,11 @@
     grids_ref, kernel_ref, prior_ref, forward_ref, backward_ref, high_ref, low_ref, out_ref, grid_ref, turned_ref
 ):
     stripe = lax.axis_index("stripe")
-    for k in range(2, 4):
+    for k in range(1, 4):
         for c in range(2):
             for column in range(0, 1024, 512):
                 tile = kernel_ref[k, c, :, column : column + 512]
-                turned_ref[k - 2, column : column + 512, c * 512 : c * 512 + 512] = tile.T
+                turned_ref[k - 1, column : column + 512, c * 512 : c * 512 + 512] = tile.T
     grids = grids_ref[...]
     modes = mm(forward_ref[...], jnp.concatenate([grids, grids], axis=0))
     prior = prior_ref[...].T
@@ -185,8 +185,8 @@
     freq = lax.broadcasted_iota(jnp.int32, (16, 1024), 0) % 4
     total = None
     for k in range(4):
-        if k >= 2:
-            term = mm(left, turned_ref[k - 2])
+        if k >= 1:
+            term = mm(left, turned_ref[k - 1])
         else:
             term = None
             for c in range(4):
@@ -278,7 +278,7 @@
         jax.ShapeDtypeStruct((4, 8, 8, 128), bf16),
         (grids, kernel, prior_spectrum.T, forward, backward, *columns),
         (whole(),) * 7,
-        (pltpu.VMEM((128, 128), f32), pltpu.VMEM((2, 1024, 1024), bf16)),
+        (pltpu.VMEM((128, 128), f32), pltpu.VMEM((3, 1024, 1024), bf16)),
         limit=20 << 20,
     )
     images = exchange(images.reshape(32, 8, 128), ("x_hi", "core", "stripe"))

time: 68.2 us -> 68 us (level)
  no operation moved by 1% of the time
where the time goes in v11:
time: 68 us; the launch traced here: 67.7 us
  blocking collectives  62.1 us (91%)
  Pallas kernels  4.79 us (7%)
  local copies, waits for them, and re-layouts  0.75 us (1%)
    all_to_all x5, blocking collectives, exchange(): return lax.all_to_all(x, axes, 0, 0, tiled=True)  62.1 us
    pallas_call x6, Pallas kernels, call(): pl.pallas_call(body, out_shape=out_shape, in_specs=list(specs), out_specs...  4.79 us

profile of v11, /device:TPU:1, one launch (start us, length us, event | category | flops | bytes accessed | tf_op | source)
XLA Modules:
  0.0 67.7 jit_solution(18159346604056064316)
XLA Ops:
  0.0 0.0 copy-start.6
  0.0 0.7 %copy-done.6 = f32[4,2,64]{2,1,0:T(2,128)S(1)} copy-done((f32[4,2,64]{2,1,0:T(2,128)S(1)}, f32[4,2,64]{2,1,0:T(2,128)}, u32[]{:S(2)}) %copy-start.6) | copy-done | bytes 2072
  0.7 0.0 copy-start.10
  0.7 0.0 slice-start
  0.7 0.1 shard_map.109
  0.8 17.4 %all_to_all.25 = f32[16,4,128]{2,1,0:T(4,128)S(1)} all-to-all(f32[16,4,128]{2,1,0:T(4,128)S(1)} %bitcast.23), channel_id=1, replica_groups=mesh['x_hi'=2,'z'=8,'core'=2,'stripe'=8] {'z','core'}, dimensions={0} | all-to-all | bytes 65536 | tf_op jit(solution)/shard_map/all_to_all | solution.py:237
  18.2 0.0 copy-done.10
  18.2 0.0 copy-start.8
  18.2 0.1 shard_map.110
  18.3 0.0 copy-start.5
  18.4 13.3 %all_to_all.26 = f32[16,8,128]{2,1,0:T(8,128)S(1)} all-to-all(f32[16,8,128]{2,1,0:T(8,128)S(1)} %bitcast.18), channel_id=1, replica_groups=mesh['x_hi'=2,'z'=8,'core'=2,'stripe'=8] {'x_hi','stripe'}, dimensions={0} | all-to-all | bytes 131072 | tf_op jit(solution)/shard_map/all_to_all | solution.py:237
  31.7 0.0 slice-done
  31.7 0.0 slice-done.1
  31.7 0.0 copy-done.2
  31.7 0.0 copy-done.3
  31.7 0.0 copy-done.8
  31.7 0.0 copy-start
  31.7 0.0 copy-start.7
  31.8 0.0 copy-start.9
  31.8 1.5 %shard_map.111 = bf16[8,16,1024]{2,1,0:T(8,128)(2,1)S(1)} custom-call(f32[2,8,8,128]{3,2,1,0:T(8,128)S(1)} %bitcast.16, bf16[4,2,512,1024]{3,2,1,0:T(8,128)(2,1)S(1)} %bitcast.13, f32[1,4]{1,0:T(1,128)S(1)} %bitcast.24, bf16[128,128]{1,0:T(8,128)(2,1)S(1)} %copy-done.3, bf16[128,128]{1,0:T(8,128)(2,1)S(1)} %copy-done.2), custom_call_target="tpu_custom_call" | custom-call | flops 1000000 | bytes 100000 | tf_op jit(solution)/shard_map/pallas_call | solution.py:21
  33.3 8.6 %all_to_all.27 = bf16[8,16,1024]{2,1,0:T(8,128)(2,1)S(1)} all-to-all(bf16[8,16,1024]{2,1,0:T(8,128)(2,1)S(1)} %shard_map.111), channel_id=1, replica_groups=mesh['x_hi'=2,'z'=8,'core'=2,'stripe'=8] {'stripe'}, dimensions={0} | all-to-all | bytes 524288 | tf_op jit(solution)/shard_map/all_to_all | solution.py:237
  41.9 0.0 copy-done.1
  41.9 0.0 copy-done.4
  41.9 0.0 copy-done.5
  41.9 2.2 %shard_map.112 = bf16[4,8,8,128]{3,2,1,0:T(8,128)(2,1)S(1)} custom-call(bf16[128,1024]{1,0:T(8,128)(2,1)S(1)} %bitcast.14, bf16[4,2,512,1024]{3,2,1,0:T(8,128)(2,1)S(1)} %bitcast.13, f32[64,128]{1,0:T(8,128)S(1)} %bitcast.21, bf16[128,256]{1,0:T(8,128)(2,1)S(1)} %copy-done.4, bf16[8,32,256]{2,1,0:T(8,128)(2,1)S(1)} %copy-done.1, ...), custom_call_target="tpu_custom_call" | custom-call | flops 1000000 | bytes 100000 | tf_op jit(solution)/shard_map/pallas_call | solution.py:21
  44.0 13.8 %all_to_all.28 = bf16[32,8,128]{2,1,0:T(8,128)(2,1)S(1)} all-to-all(bf16[32,8,128]{2,1,0:T(8,128)(2,1)S(1)} %bitcast.15), channel_id=1, replica_groups=mesh['x_hi'=2,'z'=8,'core'=2,'stripe'=8] {'x_hi','core','stripe'}, dimensions={0} | all-to-all | bytes 131072 | tf_op jit(solution)/shard_map/all_to_all | solution.py:237
  57.8 0.0 copy-done
  57.9 0.1 shard_map.113
  58.0 9.0 %all_to_all.29 = f32[8,4,128]{2,1,0:T(4,128)S(1)} all-to-all(f32[8,4,128]{2,1,0:T(4,128)S(1)} %bitcast.20), channel_id=1, replica_groups=mesh['x_hi'=2,'z'=8,'core'=2,'stripe'=8] {'z'}, dimensions={0} | all-to-all | bytes 32768 | tf_op jit(solution)/shard_map/all_to_all | solution.py:237
  67.0 0.0 copy-done.7
  67.0 0.0 copy-done.9
  67.0 0.7 %shard_map.114 = f32[4,2,64]{2,1,0:T(2,128)} custom-call(f32[32,128]{1,0:T(8,128)S(1)} %bitcast.19, f32[4,2,64]{2,1,0:T(2,128)S(1)} %copy-done.7, f32[1,64]{1,0:T(1,128)S(1)} %bitcast.25), custom_call_target="tpu_custom_call" | custom-call | flops 1000000 | bytes 100000 | tf_op jit(solution)/shard_map/pallas_call | solution.py:21
  (6 shorter events, 0.0 us)
Async XLA Ops:
  0.0 0.7 %copy-start.6 = (f32[4,2,64]{2,1,0:T(2,128)S(1)}, f32[4,2,64]{2,1,0:T(2,128)}, u32[]{:S(2)}) copy-start(f32[4,2,64]{2,1,0:T(2,128)} %data_ref.3) | copy-start | bytes 6148
  0.7 17.5 %copy-start.10 = (bf16[2,16,16,192]{3,2,1,0:T(8,128)(2,1)S(1)}, bf16[2,16,16,192]{3,2,1,0:T(8,128)(2,1)}, u32[]{:S(2)}) copy-start(bf16[2,16,16,192]{3,2,1,0:T(8,128)(2,1)} %constant.12.clone.table_ref) | copy-start | bytes 589828
  0.7 31.0 %slice-start = ((s8[8388608]{0:T(1024)(128)(4,1)}), s8[4194304]{0:T(1024)(128)(4,1)S(1)}, s32[]{:S(2)}) async-start(s8[8388608]{0:T(1024)(128)(4,1)} %bitcast.12), calls=%async_computation.5 | async-start | bytes 8388608
  18.2 13.5 %slice-start.1 = ((s8[8388608]{0:T(1024)(128)(4,1)}), s8[4194304]{0:T(1024)(128)(4,1)S(1)}, s32[]{:S(2)}) async-start(s8[8388608]{0:T(1024)(128)(4,1)} %bitcast.12), calls=%async_computation.6 | async-start | bytes 8388608
  18.2 13.5 %copy-start.2 = (bf16[128,128]{1,0:T(8,128)(2,1)S(1)}, bf16[128,128]{1,0:T(8,128)(2,1)}, u32[]{:S(2)}) copy-start(bf16[128,128]{1,0:T(8,128)(2,1)} %constant.16.clone.low_ref) | copy-start | bytes 98308
  18.2 13.5 %copy-start.3 = (bf16[128,128]{1,0:T(8,128)(2,1)S(1)}, bf16[128,128]{1,0:T(8,128)(2,1)}, u32[]{:S(2)}) copy-start(bf16[128,128]{1,0:T(8,128)(2,1)} %constant.15.clone.high_ref) | copy-start | bytes 98308
  18.2 13.5 %copy-start.8 = (f32[4]{0:T(128)S(1)}, f32[4]{0:T(128)}, u32[]{:S(2)}) copy-start(f32[4]{0:T(128)} %param.13) | copy-start | bytes 52
  18.3 23.5 %copy-start.1 = (bf16[8,32,256]{2,1,0:T(8,128)(2,1)S(1)}, bf16[8,32,256]{2,1,0:T(8,128)(2,1)}, u32[]{:S(2)}) copy-start(bf16[8,32,256]{2,1,0:T(8,128)(2,1)} %constant.14.clone.backward_ref) | copy-start | bytes 393220
  18.3 23.5 %copy-start.4 = (bf16[128,256]{1,0:T(8,128)(2,1)S(1)}, bf16[128,256]{1,0:T(8,128)(2,1)}, u32[]{:S(2)}) copy-start(bf16[128,256]{1,0:T(8,128)(2,1)} %constant.13.clone.forward_ref) | copy-start | bytes 196612
  18.3 23.5 %copy-start.5 = (f32[128,64]{0,1:T(8,128)S(1)}, f32[128,64]{0,1:T(8,128)}, u32[]{:S(2)}) copy-start(f32[128,64]{0,1:T(8,128)} %param.14) | copy-start | bytes 98308
  31.7 26.1 %copy-start = (bf16[8,4,32,96]{3,2,1,0:T(8,128)(2,1)S(1)}, bf16[8,4,32,96]{3,2,1,0:T(8,128)(2,1)}, u32[]{:S(2)}) copy-start(bf16[8,4,32,96]{3,2,1,0:T(8,128)(2,1)} %constant.17.clone.table_ref) | copy-start | bytes 589828
  31.7 35.2 %copy-start.7 = (f32[4,2,64]{2,1,0:T(2,128)S(1)}, f32[4,2,64]{2,1,0:T(2,128)}, u32[]{:S(2)}) copy-start(f32[4,2,64]{2,1,0:T(2,128)} %data_ref.3) | copy-start | bytes 6148
  31.8 35.2 %copy-start.9 = (f32[64]{0:T(128)S(1)}, f32[64]{0:T(128)}, u32[]{:S(2)}) copy-start(f32[64]{0:T(128)} %param.15) | copy-start | bytes 772
